TPU v7x, 128 devices: a whole 4x4x4 slice. The times are simulated.
128 devices in a mesh: dp: 64 (over y, x, z), tensor: 2 (over core).
Axes of the slice: x: 4, y: 4, z: 4, core: 2. Of those that a mesh axis runs over, the one named last changes fastest.
Arguments:
- tokens: bfloat16 [8192, 1024], P('dp', 'tensor'), may hold values from -6 to 6
- segment_ids: int32 [8192], P('dp'), may hold values from 0 to 7, never falling along the last dimension, each value on 1 to 2048 neighbouring positions
- valid_mask: int32 [8192], P('dp'), may hold values 0 or 1
- norm1_gain: bfloat16 [1024], replicated, may hold values from 0.099609375 to 1.8984375
- in_weight: bfloat16 [3, 1024, 1024], P(None, 'dp', 'tensor'), may hold values from -0.1875 to 0.1875
- conv_weight: bfloat16 [3, 1024], replicated, may hold values from -3.5 to 3.5
- out_weight: bfloat16 [1024, 1024], P('tensor', 'dp'), may hold values from -0.1875 to 0.1875
- norm2_gain: bfloat16 [1024], replicated, may hold values from 0.099609375 to 1.8984375
- gate_weight: bfloat16 [1024, 4608], P('dp', 'tensor'), may hold values from -0.1875 to 0.1875
- up_weight: bfloat16 [1024, 4608], P('dp', 'tensor'), may hold values from -0.1875 to 0.1875
- down_weight: bfloat16 [4608, 1024], P('tensor', 'dp'), may hold values from -0.09375 to 0.09375
- out_cotangent: bfloat16 [8192, 1024], P('dp', 'tensor'), may hold values from -6 to 6
Outputs:
- mixed_out: bfloat16 [8192, 1024], P('dp', 'tensor')
- tokens_grad: float32 [8192, 1024], P('dp', 'tensor')
- norm1_gain_grad: float32 [1024], replicated
- in_weight_grad: float32 [3, 1024, 1024], P(None, 'dp', 'tensor')
- conv_weight_grad: float32 [3, 1024], replicated
- out_weight_grad: float32 [1024, 1024], P('tensor', 'dp')
- norm2_gain_grad: float32 [1024], replicated
- gate_weight_grad: float32 [1024, 4608], P('dp', 'tensor')
- up_weight_grad: float32 [1024, 4608], P('dp', 'tensor')
- down_weight_grad: float32 [4608, 1024], P('tensor', 'dp')
All inputs are finite; a program needn't handle non-finite values. No bound on the sum of `valid_mask` on one device may be relied on, other than what follows from the above.
Results may differ from a plain program's by a relative error of at most 0.02.
Values may be sent and summed in bfloat16 or wider, within the bound.
A program may use at most 128 MiB of HBM per device.

v0:
```python
import jax
import jax.numpy as jnp
from jax import lax
from jax.sharding import PartitionSpec as P

D = 1024
KW = 3
MB = 2


EPSILON = 1e-05


def shifted(block, axis, distance):
    devices = range(lax.axis_size(axis))
    route = [(i - distance, i) for i in devices if i - distance in devices]
    return lax.ppermute(block, axis, route)


def fetch_weights(in_weight, out_weight, gate_weight, up_weight, down_weight):
    return (
        lax.all_gather(in_weight, "dp", axis=1, tiled=True),
        lax.all_gather(out_weight, "dp", axis=1, tiled=True),
        lax.all_gather(gate_weight, "dp", axis=0, tiled=True),
        lax.all_gather(up_weight, "dp", axis=0, tiled=True),
        lax.all_gather(down_weight, "dp", axis=1, tiled=True),
    )


def rms_scale(values):
    return lax.rsqrt(jnp.mean(values * values, axis=1, keepdims=True) + EPSILON)


def norm_back(grad_normed, normed_hat, scale, gain):
    weighted = grad_normed * gain
    return scale * (weighted - normed_hat * jnp.mean(weighted * normed_hat, axis=1, keepdims=True))


def tap_masks(seg_ext, valid_ext, margin, row_count):
    keep_list = []
    for offset in range(margin + 1):
        current_seg = seg_ext[margin : margin + row_count]
        earlier_seg = seg_ext[margin - offset : margin - offset + row_count]
        same_seg = (current_seg == earlier_seg).astype(jnp.int32)
        live_pair = (
            valid_ext[margin : margin + row_count]
            * valid_ext[margin - offset : margin - offset + row_count]
            * same_seg
        )
        keep_list.append(live_pair.astype(jnp.float32))
    return keep_list


def local(
    tokens,
    segment_ids,
    valid_mask,
    norm1_gain,
    in_weight,
    conv_weight,
    out_weight,
    norm2_gain,
    gate_weight,
    up_weight,
    down_weight,
    out_cotangent,
):
    margin = KW - 1
    half_width = tokens.shape[1]
    local_rows = tokens.shape[0]
    row_count = local_rows // MB
    hidden_width = gate_weight.shape[1]
    tensor_part = lax.axis_index("tensor")
    edge_tokens = shifted(tokens[local_rows - margin :], "dp", 1)
    edge_seg, edge_valid = shifted(
        (segment_ids[local_rows - margin :], valid_mask[local_rows - margin :]), "dp", 1
    )
    ext_tokens = jnp.concatenate([edge_tokens, tokens], axis=0)
    ext_seg = jnp.concatenate([edge_seg, segment_ids], axis=0)
    ext_valid = jnp.concatenate([edge_valid, valid_mask], axis=0)
    gain_one = norm1_gain.astype(jnp.float32)
    gain_two = norm2_gain.astype(jnp.float32)
    conv_local = lax.dynamic_slice_in_dim(
        conv_weight, tensor_part * half_width, half_width, 1
    ).astype(jnp.float32)
    grad_in = jnp.zeros((3, D, half_width), jnp.float32)
    grad_out = jnp.zeros((half_width, D), jnp.float32)
    grad_gate = jnp.zeros((D, hidden_width), jnp.float32)
    grad_up = jnp.zeros((D, hidden_width), jnp.float32)
    grad_down = jnp.zeros((hidden_width, D), jnp.float32)
    grad_conv = jnp.zeros((KW, half_width), jnp.float32)
    grad_gain_one = jnp.zeros((D,), jnp.float32)
    grad_gain_two = jnp.zeros((D,), jnp.float32)
    grad_ext = jnp.zeros((local_rows + margin, half_width), jnp.float32)
    outputs = []
    for micro_index in range(MB):
        current = fetch_weights(in_weight, out_weight, gate_weight, up_weight, down_weight)
        in_full, out_full, gate_full, up_full, down_full = current
        row_start = micro_index * row_count
        token_piece = ext_tokens[row_start : row_start + row_count + margin]
        grad_piece = out_cotangent[row_start : row_start + row_count]
        tap_keep = tap_masks(
            ext_seg[row_start : row_start + row_count + margin],
            ext_valid[row_start : row_start + row_count + margin],
            margin,
            row_count,
        )
        whole_tokens, whole_grad = (
            lax.all_gather(token_piece, "tensor", axis=1, tiled=True),
            lax.all_gather(grad_piece, "tensor", axis=1, tiled=True),
        )
        wide_tokens = whole_tokens.astype(jnp.float32)
        scale_one = rms_scale(wide_tokens)
        hat_one = wide_tokens * scale_one
        normed_one = (hat_one * gain_one).astype(jnp.bfloat16)
        b_part = jnp.dot(normed_one, in_full[0], preferred_element_type=jnp.float32)
        c_part = jnp.dot(normed_one, in_full[1], preferred_element_type=jnp.float32)
        v_part = jnp.dot(normed_one, in_full[2], preferred_element_type=jnp.float32)
        mixed_wide = (b_part * v_part).astype(jnp.bfloat16).astype(jnp.float32)
        conv_sum = jnp.zeros((row_count, half_width), jnp.float32)
        for offset in range(margin + 1):
            conv_sum = (
                conv_sum
                + conv_local[offset]
                * mixed_wide[margin - offset : margin - offset + row_count]
                * tap_keep[offset][:, None]
            )
        c_core = c_part[margin:]
        gated_val = (c_core * conv_sum).astype(jnp.bfloat16)
        mix_partial = jnp.dot(gated_val, out_full, preferred_element_type=jnp.float32)
        mix_share = lax.psum_scatter(
            mix_partial.astype(jnp.bfloat16), "tensor", scatter_dimension=1, tiled=True
        ).astype(jnp.float32)
        residual = token_piece[margin:].astype(jnp.float32) + mix_share
        wide_residual = lax.all_gather(
            residual.astype(jnp.bfloat16), "tensor", axis=1, tiled=True
        ).astype(residual.dtype)
        scale_two = rms_scale(wide_residual)
        hat_two = wide_residual * scale_two
        normed_two = (hat_two * gain_two).astype(jnp.bfloat16)
        gate_val = jnp.dot(normed_two, gate_full, preferred_element_type=jnp.float32)
        up_val = jnp.dot(normed_two, up_full, preferred_element_type=jnp.float32)
        sigmoid_val = jax.nn.sigmoid(gate_val)
        silu_val = gate_val * sigmoid_val
        hidden = (silu_val * up_val).astype(jnp.bfloat16)
        ffn_partial = jnp.dot(hidden, down_full, preferred_element_type=jnp.float32)
        ffn_share = lax.psum_scatter(
            ffn_partial.astype(jnp.bfloat16), "tensor", scatter_dimension=1, tiled=True
        ).astype(jnp.float32)
        outputs.append((residual + ffn_share).astype(jnp.bfloat16))
        grad_hidden = jnp.einsum(
            "rd,hd->rh", whole_grad, down_full, preferred_element_type=jnp.float32
        )
        grad_down = grad_down + jnp.einsum(
            "rh,rd->hd", hidden, whole_grad, preferred_element_type=jnp.float32
        )
        grad_gate_val = (
            grad_hidden * up_val * sigmoid_val * (1.0 + gate_val * (1.0 - sigmoid_val))
        ).astype(jnp.bfloat16)
        grad_up_val = (grad_hidden * silu_val).astype(jnp.bfloat16)
        grad_gate = grad_gate + jnp.einsum(
            "rd,rh->dh", normed_two, grad_gate_val, preferred_element_type=jnp.float32
        )
        grad_up = grad_up + jnp.einsum(
            "rd,rh->dh", normed_two, grad_up_val, preferred_element_type=jnp.float32
        )
        grad_normed_two = jnp.einsum(
            "rh,dh->rd", grad_gate_val, gate_full, preferred_element_type=jnp.float32
        ) + jnp.einsum("rh,dh->rd", grad_up_val, up_full, preferred_element_type=jnp.float32)
        grad_gain_two = grad_gain_two + jnp.sum(grad_normed_two * hat_two, axis=0)
        residual_partial = norm_back(grad_normed_two, hat_two, scale_two, gain_two)
        grad_residual = grad_piece.astype(jnp.float32) + lax.psum_scatter(
            residual_partial.astype(jnp.bfloat16), "tensor", scatter_dimension=1, tiled=True
        ).astype(jnp.float32)
        wide_grad_residual = lax.all_gather(
            grad_residual.astype(jnp.bfloat16), "tensor", axis=1, tiled=True
        )
        grad_gated = jnp.einsum(
            "rd,cd->rc", wide_grad_residual, out_full, preferred_element_type=jnp.float32
        )
        grad_out = grad_out + jnp.einsum(
            "rc,rd->cd", gated_val, wide_grad_residual, preferred_element_type=jnp.float32
        )
        grad_c = (grad_gated * conv_sum).astype(jnp.bfloat16)
        grad_conv_sum = grad_gated * c_core
        grad_mixed = jnp.zeros((row_count + margin, half_width), jnp.float32)
        conv_terms = []
        for offset in range(margin + 1):
            masked = grad_conv_sum * tap_keep[offset][:, None]
            grad_mixed = grad_mixed + jnp.pad(
                conv_local[offset] * masked, ((margin - offset, offset), (0, 0))
            )
            conv_terms.append(
                jnp.sum(masked * mixed_wide[margin - offset : margin - offset + row_count], axis=0)
            )
        grad_conv = grad_conv + jnp.stack(conv_terms)
        grad_b = (grad_mixed * v_part).astype(jnp.bfloat16)
        grad_v = (grad_mixed * b_part).astype(jnp.bfloat16)
        grad_c_ext = jnp.pad(grad_c, ((margin, 0), (0, 0)))
        grad_in = grad_in + jnp.stack(
            [
                jnp.einsum("rd,rc->dc", normed_one, grad_b, preferred_element_type=jnp.float32),
                jnp.einsum("rd,rc->dc", normed_one, grad_c_ext, preferred_element_type=jnp.float32),
                jnp.einsum("rd,rc->dc", normed_one, grad_v, preferred_element_type=jnp.float32),
            ]
        )
        grad_normed_one = jnp.einsum(
            "rc,dc->rd", grad_b, in_full[0], preferred_element_type=jnp.float32
        )
        grad_normed_one = grad_normed_one + jnp.einsum(
            "rc,dc->rd", grad_c_ext, in_full[1], preferred_element_type=jnp.float32
        )
        grad_normed_one = grad_normed_one + jnp.einsum(
            "rc,dc->rd", grad_v, in_full[2], preferred_element_type=jnp.float32
        )
        grad_gain_one = grad_gain_one + jnp.sum(grad_normed_one * hat_one, axis=0)
        token_partial = norm_back(grad_normed_one, hat_one, scale_one, gain_one)
        token_share = lax.psum_scatter(
            token_partial.astype(jnp.bfloat16), "tensor", scatter_dimension=1, tiled=True
        ).astype(jnp.float32)
        grad_ext = grad_ext.at[row_start : row_start + row_count + margin].add(token_share)
        grad_ext = grad_ext.at[row_start + margin : row_start + margin + row_count].add(
            grad_residual
        )
    edge_grad = shifted(grad_ext[:margin], "dp", -1)
    tokens_grad = grad_ext[margin:]
    tokens_grad = tokens_grad.at[local_rows - margin :].add(edge_grad)
    in_total, out_total, gate_total, up_total, down_total = (
        lax.psum_scatter(grad_in, "dp", scatter_dimension=1, tiled=True),
        lax.psum_scatter(grad_out, "dp", scatter_dimension=1, tiled=True),
        lax.psum_scatter(grad_gate, "dp", scatter_dimension=0, tiled=True),
        lax.psum_scatter(grad_up, "dp", scatter_dimension=0, tiled=True),
        lax.psum_scatter(grad_down, "dp", scatter_dimension=1, tiled=True),
    )
    conv_full = lax.dynamic_update_slice_in_dim(
        jnp.zeros((KW, D), jnp.float32), grad_conv, tensor_part * half_width, 1
    )
    conv_total, gain_one_total, gain_two_total = lax.psum(
        (conv_full, grad_gain_one, grad_gain_two), ("dp", "tensor")
    )
    return (
        jnp.concatenate(outputs, axis=0),
        tokens_grad,
        gain_one_total,
        in_total,
        conv_total,
        out_total,
        gain_two_total,
        gate_total,
        up_total,
        down_total,
    )


def solution(mesh):
    placed = (
        P("dp", "tensor"),
        P("dp"),
        P("dp"),
        P(),
        P(None, "dp", "tensor"),
        P(),
        P("tensor", "dp"),
        P(),
        P("dp", "tensor"),
        P("dp", "tensor"),
        P("tensor", "dp"),
        P("dp", "tensor"),
    )
    return jax.shard_map(
        local,
        mesh=mesh,
        in_specs=placed,
        out_specs=(
            P("dp", "tensor"),
            P("dp", "tensor"),
            P(),
            P(None, "dp", "tensor"),
            P(),
            P("tensor", "dp"),
            P(),
            P("dp", "tensor"),
            P("dp", "tensor"),
            P("tensor", "dp"),
        ),
        check_vma=False,
    )
```

profile of v0, /device:TPU:0, one launch (start us, length us, event | category | flops | bytes accessed | tf_op | source)
XLA Modules:
  0.0 1889.0 jit_solution(17313688936250836257)
XLA Ops:
  8.7 3.9 collective-permute-start.2
  13.3 3.8 collective-permute-start.1
  17.8 3.5 collective-permute-start
  31.1 49.7 %all-gather.6.cloned.1.call-done = bf16[3,1024,512]{2,1,0:T(8,128)(2,1)} async-done(((bf16[3,16,512]{2,1,0:T(8,128)(2,1)}), bf16[3,1024,512]{2,1,0:T(8,128)(2,1)}) %all-gather.6.cloned.1.call-update) | async-done | bytes 3145744 | tf_op jit(solution)/shard_map/all_gather | solution.py:22
  90.7 55.0 %all-gather.8.cloned.1.call-done = bf16[512,1024]{0,1:T(8,128)(2,1)} async-done(((bf16[512,16]{0,1:T(8,128)(2,1)}), bf16[512,1024]{0,1:T(8,128)(2,1)}) %all-gather.8.cloned.1.call-update) | async-done | bytes 1048592 | tf_op jit(solution)/shard_map/all_gather | solution.py:23
  158.0 11.9 reduce-scatter.18.cloned.1.call-done
  176.1 67.7 %all-gather.10.cloned.1.call-done = bf16[1024,2304]{1,0:T(8,128)(2,1)} async-done(((bf16[16,2304]{1,0:T(8,128)(2,1)}), bf16[1024,2304]{1,0:T(8,128)(2,1)}) %all-gather.10.cloned.1.call-update) | async-done | bytes 4718608 | tf_op jit(solution)/shard_map/all_gather | solution.py:24
  243.8 4.2 fusion.80
  248.0 65.6 %all-gather.12.cloned.1.call-done = bf16[1024,2304]{1,0:T(8,128)(2,1)} async-done(((bf16[16,2304]{1,0:T(8,128)(2,1)}), bf16[1024,2304]{1,0:T(8,128)(2,1)}) %all-gather.12.cloned.1.call-update) | async-done | bytes 4718608 | tf_op jit(solution)/shard_map/all_gather | solution.py:25
  313.6 4.2 fusion.78
  317.8 65.8 %all-gather.14.cloned.1.call-done = bf16[2304,1024]{0,1:T(8,128)(2,1)} async-done(((bf16[2304,16]{0,1:T(8,128)(2,1)}), bf16[2304,1024]{0,1:T(8,128)(2,1)}) %all-gather.14.cloned.1.call-update) | async-done | bytes 4718608 | tf_op jit(solution)/shard_map/all_gather | solution.py:26
  383.6 4.5 multiply_convert_fusion
  402.8 4.6 convolution_convert_fusion.2
  407.6 4.6 convolution_convert_fusion
  412.4 9.4 reduce-scatter.22.cloned.1.call-done
  453.0 5.2 convolution_add_fusion.2
  460.7 5.1 convolution_add_fusion.1
  468.2 5.0 convolution_add_fusion
  481.7 71.6 %all-reduce.9 = (f32[1024]{0:T(1024)}, f32[3,1024]{1,0:T(4,128)}, f32[1024]{0:T(1024)}) all-reduce(f32[1024]{0:T(1024)S(1)} %add.248, f32[3,1024]{1,0:T(4,128)S(1)} %fusion.66, f32[1024]{0:T(1024)S(1)} %add.252), channel_id=1, replica_groups=mesh['dp'=64,'tensor'=2] {'dp','tensor'}, use_global_device_ids=true, to_apply=%region_18.19 | all-reduce | flops 5120 | bytes 40960 | tf_op jit(solution)/shard_map/psum | solution.py:238
  553.4 282.2 %reduce-scatter.32.cloned.1.call-done = f32[512,16]{0,1:T(8,128)} async-done(((f32[512,1024]{0,1:T(8,128)}), f32[512,16]{0,1:T(8,128)}) %reduce-scatter.32.cloned.1.call-update) | async-done | bytes 32784 | tf_op jit(solution)/shard_map/reduce_scatter | solution.py:230
  835.7 360.1 %reduce-scatter.30.cloned.1.call-done = f32[3,16,512]{2,1,0:T(8,128)} async-done(((f32[3,1024,512]{2,1,0:T(8,128)}), f32[3,16,512]{2,1,0:T(8,128)}) %reduce-scatter.30.cloned.1.call-update) | async-done | bytes 98320 | tf_op jit(solution)/shard_map/reduce_scatter | solution.py:229
  1195.8 226.8 %reduce-scatter.34.cloned.1.call-done = f32[16,2304]{1,0:T(8,128)} async-done(((f32[1024,2304]{1,0:T(8,128)}), f32[16,2304]{1,0:T(8,128)}) %reduce-scatter.34.cloned.1.call-update) | async-done | bytes 147472 | tf_op jit(solution)/shard_map/reduce_scatter | solution.py:231
  1422.6 230.1 %reduce-scatter.36.cloned.1.call-done = f32[16,2304]{1,0:T(8,128)} async-done(((f32[1024,2304]{1,0:T(8,128)}), f32[16,2304]{1,0:T(8,128)}) %reduce-scatter.36.cloned.1.call-update) | async-done | bytes 147472 | tf_op jit(solution)/shard_map/reduce_scatter | solution.py:232
  1652.7 229.4 %reduce-scatter.38.cloned.1.call-done = f32[2304,16]{0,1:T(8,128)} async-done(((f32[2304,1024]{0,1:T(8,128)}), f32[2304,16]{0,1:T(8,128)}) %reduce-scatter.38.cloned.1.call-update) | async-done | bytes 147472 | tf_op jit(solution)/shard_map/reduce_scatter | solution.py:233
  (332 shorter events, 99.4 us)
Async XLA Ops:
  7.2 73.6 %all-gather.6.cloned.1.call-start = ((), (), s32[]{:S(2)}) async-start(), calls=%async_computation.13 | async-start | bytes 3194880 | tf_op jit(solution)/shard_map/all_gather | solution.py:22
  7.9 137.8 %all-gather.8.cloned.1.call-start = ((), (), s32[]{:S(2)}) async-start(), calls=%async_computation.14 | async-start | bytes 1064960 | tf_op jit(solution)/shard_map/all_gather | solution.py:23
  8.7 14.2 collective-permute-start.2
  13.3 10.3 collective-permute-start.1
  17.8 7.5 collective-permute-start
  21.4 136.6 %reduce-scatter.14.cloned.1.call-start = ((), (), s32[]{:S(2)}) async-start(), calls=%async_computation.15 | async-start | bytes 196608 | tf_op jit(solution)/shard_map/reduce_scatter | solution.py:131
  90.7 82.2 %copy-start.48 = (bf16[64,512]{1,0:T(8,128)(2,1)}, bf16[64,512]{1,0:T(8,128)(2,1)S(1)}, u32[]{:S(2)}) copy-start(bf16[64,512]{1,0:T(8,128)(2,1)S(1)} %get-tuple-element.129) | copy-start | bytes 196612
  148.1 21.8 %reduce-scatter.18.cloned.1.call-start = ((), (), s32[]{:S(2)}) async-start(), calls=%async_computation.20 | async-start | bytes 196608 | tf_op jit(solution)/shard_map/reduce_scatter | solution.py:131
  150.5 93.3 %all-gather.10.cloned.1.call-start = ((), (), s32[]{:S(2)}) async-start(), calls=%async_computation.16 | async-start | bytes 4792320 | tf_op jit(solution)/shard_map/all_gather | solution.py:24
  151.1 162.5 %all-gather.12.cloned.1.call-start = ((), (), s32[]{:S(2)}) async-start(), calls=%async_computation.17 | async-start | bytes 4792320 | tf_op jit(solution)/shard_map/all_gather | solution.py:25
  151.7 231.9 %all-gather.14.cloned.1.call-start = ((), (), s32[]{:S(2)}) async-start(), calls=%async_computation.18 | async-start | bytes 4792320 | tf_op jit(solution)/shard_map/all_gather | solution.py:26
  152.4 259.9 %reduce-scatter.26.cloned.1.call-start = ((), (), s32[]{:S(2)}) async-start(), calls=%async_computation.24 | async-start | bytes 196608 | tf_op jit(solution)/shard_map/reduce_scatter | solution.py:172
  400.3 21.4 %reduce-scatter.22.cloned.1.call-start = ((), (), s32[]{:S(2)}) async-start(), calls=%async_computation.22 | async-start | bytes 196608 | tf_op jit(solution)/shard_map/reduce_scatter | solution.py:172
  402.7 71.2 %reduce-scatter.16.cloned.1.call-start = ((), (), s32[]{:S(2)}) async-start(), calls=%async_computation.19 | async-start | bytes 196608 | tf_op jit(solution)/shard_map/reduce_scatter | solution.py:147
  407.4 66.5 %reduce-scatter.20.cloned.1.call-start = ((), (), s32[]{:S(2)}) async-start(), calls=%async_computation.21 | async-start | bytes 196608 | tf_op jit(solution)/shard_map/reduce_scatter | solution.py:147
  412.3 63.5 %reduce-scatter.24.cloned.1.call-start = ((), (), s32[]{:S(2)}) async-start(), calls=%async_computation.23 | async-start | bytes 221184 | tf_op jit(solution)/shard_map/reduce_scatter | solution.py:218
  439.7 38.9 %reduce-scatter.28.cloned.1.call-start = ((), (), s32[]{:S(2)}) async-start(), calls=%async_computation.25 | async-start | bytes 221184 | tf_op jit(solution)/shard_map/reduce_scatter | solution.py:218
  441.3 394.4 %reduce-scatter.32.cloned.1.call-start = ((), (), s32[]{:S(2)}) async-start(), calls=%async_computation.27 | async-start | bytes 2129920 | tf_op jit(solution)/shard_map/reduce_scatter | solution.py:230
  444.2 751.6 %reduce-scatter.30.cloned.1.call-start = ((), (), s32[]{:S(2)}) async-start(), calls=%async_computation.26 | async-start | bytes 6389760 | tf_op jit(solution)/shard_map/reduce_scatter | solution.py:229
  450.6 972.0 %reduce-scatter.34.cloned.1.call-start = ((), (), s32[]{:S(2)}) async-start(), calls=%async_computation.28 | async-start | bytes 9584640 | tf_op jit(solution)/shard_map/reduce_scatter | solution.py:231
  458.2 1194.5 %reduce-scatter.36.cloned.1.call-start = ((), (), s32[]{:S(2)}) async-start(), calls=%async_computation.29 | async-start | bytes 9584640 | tf_op jit(solution)/shard_map/reduce_scatter | solution.py:232
  465.8 1416.4 %reduce-scatter.38.cloned.1.call-start = ((), (), s32[]{:S(2)}) async-start(), calls=%async_computation.30 | async-start | bytes 9584640 | tf_op jit(solution)/shard_map/reduce_scatter | solution.py:233
  480.3 73.1 %collective-permute-start.3 = (f32[2,512]{1,0:T(2,128)S(1)}, f32[2,512]{1,0:T(2,128)S(1)}, u32[]{:S(2)}, u32[]{:S(2)}) collective-permute-start(f32[2,512]{1,0:T(2,128)S(1)} %slice.326), channel_id=1, source_target_pairs={{2,0},{4,2},{6,4},{8,6},{10,8},{12,10},{14,12},{16,14},{18,16},{20... | collective-permute-start | bytes 12296 | tf_op jit(solution)/shard_map/ppermute | solution.py:17
  553.4 1328.8 %copy-start.49 = (f32[128,512]{1,0:T(8,128)}, f32[128,512]{1,0:T(8,128)S(1)}, u32[]{:S(2)}) copy-start(f32[128,512]{1,0:T(8,128)S(1)} %fusion.67) | copy-start | bytes 786436
  (94 other events, 1333.7 us)
Sparse Core Ops, SparseCore 0:
  10.9 69.8 all-gather.5
  83.7 61.9 all-gather.7
  148.6 7.4 reduce-scatter.13
  158.3 11.5 reduce-scatter.17
  172.6 71.2 all-gather.9
  246.5 67.0 all-gather.11
  316.4 67.0 all-gather.13
  400.4 7.3 reduce-scatter.25
  410.2 11.5 reduce-scatter.21
  423.9 11.5 reduce-scatter.15
  437.8 11.5 reduce-scatter.19
  451.5 11.5 reduce-scatter.23
  466.0 11.5 reduce-scatter.27
  480.4 355.2 reduce-scatter.31
  838.6 357.1 reduce-scatter.29
  1200.8 221.7 reduce-scatter.33
  1428.3 224.4 reduce-scatter.35
  1657.7 224.3 reduce-scatter.37
where the time goes:
time: 1890 us
  waiting for transfers between devices  1660 us (88%)
  blocking collectives  87.2 us (5%)
  matrix products  81.9 us (4%)
  other arithmetic  23.4 us (1%)
    reduce_scatter x1, waiting for transfers between devices, local(): lax.psum_scatter(grad_in, 'dp', scatter_dimension=1, tiled=True)  360 us
    reduce_scatter x1, waiting for transfers between devices, local(): lax.psum_scatter(grad_out, 'dp', scatter_dimension=1, tiled=True)  282 us
    reduce_scatter x1, waiting for transfers between devices, local(): lax.psum_scatter(grad_up, 'dp', scatter_dimension=0, tiled=True)  230 us
    reduce_scatter x1, waiting for transfers between devices, local(): lax.psum_scatter(grad_down, 'dp', scatter_dimension=1, tiled=True)  229 us
    reduce_scatter x1, waiting for transfers between devices, local(): lax.psum_scatter(grad_gate, 'dp', scatter_dimension=0, tiled=True)  227 us
    psum x1, blocking collectives, local(): lax.psum((conv_full, grad_gain_one, grad_gain_two), ('dp', 'tensor'))  71.6 us
    all_gather x1, waiting for transfers between devices, fetch_weights(): lax.all_gather(gate_weight, 'dp', axis=0, tiled=True)  67.7 us
    all_gather x1, waiting for transfers between devices, fetch_weights(): lax.all_gather(down_weight, 'dp', axis=1, tiled=True)  65.8 us
  transfers between devices with their start and end apart: 22, of which 12 were waited for; matrix products, arithmetic and copies ran while one was open for 5% of the time, Pallas kernels for 0%

commit v1 on v0

v1 whole, which is shorter than its diff:
```python
import jax
import jax.numpy as jnp
from jax import lax
from jax.experimental import pallas as pl
from jax.experimental.pallas import tpu as pltpu
from jax.sharding import PartitionSpec as P

D = 1024
EPS = 1e-05
R = 4
BF = jnp.bfloat16
F32 = jnp.float32
TOK = 128
GT = 512
HALF = 512
CH = 128
HID = 576
HP = 640
WIDTHS = (512, 2 * HP, HP)
NCOPY = 230


def nn(a, b):
    return lax.dot_general(a, b, (((1,), (0,)), ((), ())), preferred_element_type=F32)


def nt(a, b):
    return lax.dot_general(a, b, (((1,), (1,)), ((), ())), preferred_element_type=F32)


def tn(a, b):
    return lax.dot_general(a, b, (((0,), (0,)), ((), ())), preferred_element_type=F32)


def add_into(dst, *others):
    total = dst[...].astype(F32)
    for other in others:
        total = total + other[...].astype(F32)
    dst[...] = total.astype(dst.dtype)


class Wire:
    def __init__(self, send_sems, recv_sems):
        self.send_sems, self.recv_sems, self.started = send_sems, recv_sems, []

    def send(self, src, dst, device):
        k = len(self.started)
        copy = pltpu.make_async_remote_copy(
            src_ref=src,
            dst_ref=dst,
            send_sem=self.send_sems.at[k],
            recv_sem=self.recv_sems.at[k],
            device_id=device,
            device_id_type=pl.DeviceIdType.MESH,
        )
        copy.start()
        self.started.append(copy)
        return copy

    def finish(self):
        for copy in self.started:
            copy.wait_send()


def ring_ag(wire, i, plus, minus, blk):
    prev, nxt = (i + R - 1) % R, (i + 1) % R
    c1 = wire.send(blk(i, None), blk(i, None), plus)
    c2 = wire.send(blk(i, None), blk(i, None), minus)
    yield
    c1.wait_recv()
    c3 = wire.send(blk(prev, 0), blk(prev, 0), plus)
    c2.wait_recv()
    c4 = wire.send(blk(nxt, 1), blk(nxt, 1), minus)
    yield
    c3.wait_recv()
    c4.wait_recv()
    yield


def ring_rs(wire, i, plus, minus, blk, recv):
    prev, nxt, far = (i + R - 1) % R, (i + 1) % R, (i + 2) % R
    c1 = wire.send(blk(far, 0), recv[0], plus)
    c2 = wire.send(blk(far, 1), recv[1], minus)
    c3 = wire.send(blk(nxt, 1), recv[2], plus)
    c4 = wire.send(blk(prev, 0), recv[3], minus)
    yield
    c1.wait_recv()
    add_into(blk(nxt, 0), recv[0])
    c5 = wire.send(blk(nxt, 0), recv[4], plus)
    c2.wait_recv()
    add_into(blk(prev, 1), recv[1])
    c6 = wire.send(blk(prev, 1), recv[5], minus)
    yield
    for c in (c3, c4, c5, c6):
        c.wait_recv()
    yield


def together(*gens):
    for _ in zip(*gens):
        yield


def kernel(
    tok_ref,
    dy_ref,
    code_ref,
    vec_ref,
    pack0,
    pack1,
    pack2,
    mix_out,
    tg_out,
    small_out,
    g0_out,
    g1_out,
    g2_out,
    w0,
    w1,
    w2,
    g0,
    g1,
    g2,
    ra0,
    ra1,
    ra2,
    rb0,
    rb1,
    rb2,
    oa0,
    oa1,
    oa2,
    codes,
    n1,
    dyf,
    n2,
    dhb,
    zpart,
    zrc,
    zp,
    zr,
    stat_s,
    stat_r,
    hat1,
    hat2,
    h2s,
    dh2s,
    bcv,
    dbcv,
    zc,
    gat,
    mx,
    cd,
    q1,
    q2,
    halo_s,
    halo_r,
    uu,
    dab,
    red,
    send_sems,
    recv_sems,
):
    dp = lax.axis_index("dp")
    core = lax.axis_index("tensor")
    y, x, z = dp // 16, (dp // 4) % 4, dp % 4
    group = dp // 4

    def dev(yy, xx, zz):
        return (yy * 16 + xx * 4 + zz, core)

    def up(v, k=1):
        return (v + k) % R

    peer = (dp, 1 - core)
    xs = [None] + [dev(y, up(x, k), z) for k in (1, 2, 3)]
    ys = [None] + [dev(up(y, k), x, z) for k in (1, 2, 3)]
    zs = [None] + [dev(y, x, up(z, k)) for k in (1, 2, 3)]
    after = ((dp + 4) % 64, core)
    before = ((dp + 60) % 64, core)

    barrier = pltpu.get_barrier_semaphore()
    others = [peer, after, before] + xs[1:] + ys[1:] + zs[1:]
    for other in others:
        pl.semaphore_signal(barrier, inc=1, device_id=other, device_id_type=pl.DeviceIdType.MESH)
    pl.semaphore_wait(barrier, len(others))

    wire = Wire(send_sems, recv_sems)
    packs, ws, gs = (pack0, pack1, pack2), (w0, w1, w2), (g0, g1, g2)
    ras, rbs, oas = (ra0, ra1, ra2), (rb0, rb1, rb2), (oa0, oa1, oa2)
    my_cols = pl.ds(pl.multiple_of(core * HALF, HALF), HALF)
    peer_cols = pl.ds(pl.multiple_of((1 - core) * HALF, HALF), HALF)

    def rows_of(j, count=TOK):
        return pl.ds(pl.multiple_of(j * count, count), count)

    def scatter_weights(c):
        mine = pl.ds(pl.multiple_of(z * 16, 16), 16)
        slab = ws[c].at[y, x, mine, :]
        copies = [wire.send(packs[c].at[up(z, k)], slab, zs[k]) for k in (1, 2, 3)]
        ws[c][y, x, mine, :] = packs[c][z]
        return copies

    def ag_plane(c):
        w = ws[c]

        def part(base, h):
            return pl.ds(base, 32) if h is None else pl.ds(base + 16 * h, 16)

        yield from together(
            ring_ag(wire, x, xs[1], xs[3], lambda j, h: w.at[y, j, part(0, h), :]),
            ring_ag(wire, y, ys[1], ys[3], lambda j, h: w.at[j, x, part(32, h), :]),
        )
        yield from together(
            ring_ag(wire, y, ys[1], ys[3], lambda j, h: w.at[j, :, part(0, h), :]),
            ring_ag(wire, x, xs[1], xs[3], lambda j, h: w.at[:, j, part(32, h), :]),
        )

    def rs_plane(c):
        g, ra, rb = gs[c], ras[c], rbs[c]

        def part(base, h):
            return pl.ds(base + 16 * h, 16)

        yield from together(
            ring_rs(wire, y, ys[1], ys[3], lambda j, h: g.at[j, :, part(0, h), :], [ra.at[0, k] for k in range(6)]),
            ring_rs(wire, x, xs[1], xs[3], lambda j, h: g.at[:, j, part(32, h), :], [ra.at[1, k] for k in range(6)]),
        )
        for h, (u, v) in ((0, (3, 4)), (1, (2, 5))):
            add_into(g.at[y, :, part(0, h), :], ra.at[0, u], ra.at[0, v])
            add_into(g.at[:, x, part(32, h), :], ra.at[1, u], ra.at[1, v])
        yield from together(
            ring_rs(wire, x, xs[1], xs[3], lambda j, h: g.at[y, j, part(0, h), :], [rb.at[0, k] for k in range(6)]),
            ring_rs(wire, y, ys[1], ys[3], lambda j, h: g.at[j, x, part(32, h), :], [rb.at[1, k] for k in range(6)]),
        )
        for h, (u, v) in ((0, (3, 4)), (1, (2, 5))):
            add_into(g.at[y, x, part(0, h), :], rb.at[0, u], rb.at[0, v])
            add_into(g.at[y, x, part(32, h), :], rb.at[1, u], rb.at[1, v])
        yield

    def gather_grads(c):
        def rows(j):
            return gs[c].at[y, x, pl.ds(pl.multiple_of(j * 16, 16), 16), :]

        copies = [wire.send(rows(up(z, k)), oas[c].at[z], zs[k]) for k in (1, 2, 3)]
        oas[c][z] = rows(z)[...]
        return copies

    def ag_group(n):
        def blk(j, h):
            base, count = (0, TOK) if h is None else (h * (TOK // 2), TOK // 2)
            return n.at[pl.ds(pl.multiple_of(j * TOK + base, TOK // 2), count), my_cols]

        def both(j, h, device):
            return wire.send(blk(j, h), blk(j, h), device)

        prev, nxt, far = up(z, 3), up(z), up(z, 2)
        c1 = both(z, None, zs[1])
        c2 = both(z, None, zs[3])
        got = [both(z, None, peer)]
        yield
        c1.wait_recv()
        c3 = both(prev, 0, zs[1])
        got.append(both(prev, None, peer))
        c2.wait_recv()
        c4 = both(nxt, 1, zs[3])
        got.append(both(nxt, None, peer))
        yield
        c3.wait_recv()
        got.append(both(far, 0, peer))
        c4.wait_recv()
        got.append(both(far, 1, peer))
        yield
        for c in got:
            c.wait_recv()
        yield

    def rs_group(k):
        part, rc, p = zpart.at[k], zrc.at[k], zp.at[k]
        c = wire.send(part.at[:, peer_cols], rc, peer)
        yield
        c.wait_recv()
        p[...] = (part[:, my_cols].astype(F32) + rc[...].astype(F32)).astype(BF)

        def blk(j, h):
            return p.at[pl.ds(pl.multiple_of(j * TOK + h * (TOK // 2), TOK // 2), TOK // 2), :]

        yield from ring_rs(wire, z, zs[1], zs[3], blk, [zr.at[k, i] for i in range(6)])

    def rs_result(k):
        def half(h, u, v):
            own = zp[k, pl.ds(pl.multiple_of(z * TOK + h * (TOK // 2), TOK // 2), TOK // 2), :]
            return own.astype(F32) + zr[k, u].astype(F32) + zr[k, v].astype(F32)

        return jnp.concatenate([half(0, 3, 4), half(1, 2, 5)], axis=0)

    def chip_sum(k, values):
        stat_s[k] = jnp.broadcast_to(jnp.sum(values, axis=1, keepdims=True), (TOK, CH))
        c = wire.send(stat_s.at[k], stat_r.at[k], peer)
        c.wait_recv()
        return (stat_s[k] + stat_r[k])[:, :1]

    dealt0 = scatter_weights(0)
    tok = tok_ref[...].astype(F32)
    r1 = lax.rsqrt(chip_sum(0, tok * tok) * (1.0 / D) + EPS)
    gain1 = vec_ref[pl.ds(0, 1), my_cols]
    gain2 = vec_ref[pl.ds(1, 1), my_cols]
    hat1[...] = tok * r1
    n1[rows_of(z), my_cols] = (hat1[...] * gain1).astype(BF)
    ag_n1 = ag_group(n1)
    next(ag_n1)
    codes[z] = code_ref[...]
    code_copies = [wire.send(code_ref, codes.at[z], zs[k]) for k in (1, 2, 3)]
    for c in dealt0:
        c.wait_recv()
    ag0 = ag_plane(0)
    next(ag0)
    dealt1 = scatter_weights(1)
    dealt2 = scatter_weights(2)
    next(ag_n1)
    next(ag0)
    next(ag0)
    for c in dealt1:
        c.wait_recv()
    ag1 = ag_plane(1)
    next(ag0)
    next(ag1)
    next(ag_n1)
    dyf[rows_of(z), my_cols] = dy_ref[...]
    ag_dy = ag_group(dyf)
    next(ag_dy)
    next(ag0)
    for c in dealt2:
        c.wait_recv()
    ag2 = ag_plane(2)
    next(ag2)
    next(ag1)
    next(ag_n1)
    next(ag0)

    ch_cols = pl.ds(pl.multiple_of(core * HALF + z * CH, CH), CH)
    taps = [vec_ref[pl.ds(2 + k, 1), ch_cols] for k in range(3)]
    bcv[...] = nn(n1[...], w0[...].reshape(D, 512)[:, : 3 * CH])
    mx[pl.ds(8, GT), :] = (bcv[:, 0:CH] * bcv[:, 2 * CH : 3 * CH]).astype(BF).astype(F32)
    for c in code_copies:
        c.wait_recv()
    cd[pl.ds(8, GT), :] = codes[...].reshape(GT, CH).astype(F32)
    halo_s[0, 0] = mx[pl.ds(GT, 8), :]
    halo_s[0, 1] = cd[pl.ds(GT, 8), :]
    c = wire.send(halo_s.at[0], halo_r.at[0], after)
    next(ag1)
    next(ag2)
    next(ag_dy)
    c.wait_recv()
    first = group == 0
    mx[pl.ds(0, 8), :] = halo_r[0, 0]
    cd[pl.ds(0, 8), :] = jnp.where(first, -1.0, halo_r[0, 1])
    code = cd[pl.ds(8, GT), :]
    live = code >= 16.0

    def keep(k):
        return jnp.where(live & (code == cd[pl.ds(8 - k, GT), :]), 1.0, 0.0)

    zc[...] = (
        taps[0] * mx[pl.ds(8, GT), :] * keep(0)
        + taps[1] * mx[pl.ds(7, GT), :] * keep(1)
        + taps[2] * mx[pl.ds(6, GT), :] * keep(2)
    )
    gat[...] = (bcv[:, CH : 2 * CH] * zc[...]).astype(BF)

    @pl.loop(0, 2)
    def _(i):
        rows = rows_of(i, 256)
        zpart[0, rows, :] = nt(gat[rows, :], w0[...].reshape(D, 512)[:, 3 * CH :]).astype(BF)

    rs_y = rs_group(0)
    next(rs_y)
    next(ag1)
    next(ag2)
    next(rs_y)
    next(ag_dy)
    next(rs_y)
    next(ag1)
    next(ag2)
    next(rs_y)
    h2s[...] = tok_ref[...].astype(F32) + rs_result(0)
    h2 = h2s[...]
    r2 = lax.rsqrt(chip_sum(1, h2 * h2) * (1.0 / D) + EPS)
    hat2[...] = h2 * r2
    n2[rows_of(z), my_cols] = (hat2[...] * gain2).astype(BF)
    ag_n2 = ag_group(n2)
    next(ag_n2)
    next(ag2)
    next(ag_n2)
    next(ag1)
    next(ag_dy)
    next(ag_n2)
    next(ag2)
    next(ag_n2)

    @pl.loop(0, 2)
    def _(i):
        rows = rows_of(i, 256)
        ab = nn(n2[rows, :], w1[...].reshape(D, 2 * HP))
        a, b = ab[:, :HP], ab[:, HP:]
        s = jax.nn.sigmoid(a)
        silu = a * s
        uu[rows, :] = (silu * b).astype(BF)
        du = nn(dyf[rows, :], w2[...].reshape(D, HP))
        dab[rows, 0:HP] = (du * b * s * (1.0 + a * (1.0 - s))).astype(BF)
        dab[rows, HP : 2 * HP] = (du * silu).astype(BF)

    @pl.loop(0, 2)
    def _(i):
        rows = rows_of(i, 256)
        zpart[1, rows, :] = nt(dab[rows, :], w1[...].reshape(D, 2 * HP)).astype(BF)

    rs_n2 = rs_group(1)
    next(rs_n2)

    @pl.loop(0, 4)
    def _(i):
        cols = rows_of(i, 256)
        g1[i] = tn(n2[:, cols], dab[...]).astype(BF).reshape(4, 64, 2 * HP)

    next(rs_n2)
    rs1 = rs_plane(1)
    next(rs1)
    next(rs_n2)

    @pl.loop(0, 4)
    def _(i):
        cols = rows_of(i, 256)
        g2[i] = tn(dyf[:, cols], uu[...]).astype(BF).reshape(4, 64, HP)

    next(rs_n2)
    rs2 = rs_plane(2)
    dn2 = rs_result(1)
    small_out[...] = jnp.zeros((8, D), F32)
    small_out[pl.ds(1, 1), my_cols] = jnp.sum(dn2 * hat2[...], axis=0, keepdims=True)
    e2 = dn2 * gain2
    m2 = chip_sum(2, e2 * hat2[...]) * (1.0 / D)
    dh2s[...] = dy_ref[...].astype(F32) + r2 * (e2 - hat2[...] * m2)
    dhb[rows_of(z), my_cols] = dh2s[...].astype(BF)
    ag_dh = ag_group(dhb)
    next(ag_dh)
    next(rs2)
    next(rs1)
    next(ag_dh)

    @pl.loop(0, 2)
    def _(i):
        rows = rows_of(i, 256)
        zpart[2, rows, :] = nt(uu[rows, :], w2[...].reshape(D, HP)).astype(BF)

    rs_u = rs_group(2)
    next(ag_dh)
    next(rs_u)
    next(ag_dh)

    dg = nn(dhb[...], w0[...].reshape(D, 512)[:, 3 * CH :])
    dbcv[:, CH : 2 * CH] = (dg * zc[...]).astype(BF)
    dz = dg * bcv[:, CH : 2 * CH]
    code = cd[pl.ds(8, GT), :]
    live = code >= 16.0
    q0 = dz * keep(0)
    q1[pl.ds(0, GT), :] = dz * keep(1)
    q2[pl.ds(0, GT), :] = dz * keep(2)
    halo_s[1, 0] = q1[pl.ds(0, 8), :]
    halo_s[1, 1] = q2[pl.ds(0, 8), :]
    c = wire.send(halo_s.at[1], halo_r.at[1], before)
    small_out[pl.ds(2, 1), ch_cols] = jnp.sum(q0 * mx[pl.ds(8, GT), :], axis=0, keepdims=True)
    small_out[pl.ds(3, 1), ch_cols] = jnp.sum(q1[pl.ds(0, GT), :] * mx[pl.ds(7, GT), :], axis=0, keepdims=True)
    small_out[pl.ds(4, 1), ch_cols] = jnp.sum(q2[pl.ds(0, GT), :] * mx[pl.ds(6, GT), :], axis=0, keepdims=True)
    c.wait_recv()
    last = group == 15
    q1[pl.ds(GT, 8), :] = jnp.where(last, 0.0, halo_r[1, 0])
    q2[pl.ds(GT, 8), :] = jnp.where(last, 0.0, halo_r[1, 1])
    dm = taps[0] * q0 + taps[1] * q1[pl.ds(1, GT), :] + taps[2] * q2[pl.ds(2, GT), :]
    dbcv[:, 0:CH] = (dm * bcv[:, 2 * CH : 3 * CH]).astype(BF)
    dbcv[:, 2 * CH : 3 * CH] = (dm * bcv[:, 0:CH]).astype(BF)

    @pl.loop(0, 2)
    def _(i):
        rows = rows_of(i, 256)
        zpart[3, rows, :] = nt(dbcv[rows, :], w0[...].reshape(D, 512)[:, : 3 * CH]).astype(BF)

    rs_n1 = rs_group(3)
    next(rs_n1)
    next(rs1)
    next(rs2)

    @pl.loop(0, 4)
    def _(i):
        cols = rows_of(i, 256)
        g0[i, :, :, 0 : 3 * CH] = tn(n1[:, cols], dbcv[...]).astype(BF).reshape(4, 64, 3 * CH)
        g0[i, :, :, 3 * CH : 4 * CH] = tn(dhb[:, cols], gat[...]).astype(BF).reshape(4, 64, CH)

    rs0 = rs_plane(0)
    next(rs0)
    next(rs_n1)
    next(rs_u)
    next(rs_n1)
    next(rs0)
    next(rs2)
    next(rs_u)
    next(rs_n1)

    dn1 = rs_result(3)
    small_out[pl.ds(0, 1), my_cols] = jnp.sum(dn1 * hat1[...], axis=0, keepdims=True)
    e1 = dn1 * gain1
    m1 = chip_sum(3, e1 * hat1[...]) * (1.0 / D)
    tg_out[...] = dh2s[...] + r1 * (e1 - hat1[...] * m1)

    def all_sum(k, i, peers):
        red[k, i] = small_out[...]
        copies = [wire.send(red.at[k, i], red.at[k, i], peers[j]) for j in (1, 2, 3)]
        yield
        for c in copies:
            c.wait_recv()
        small_out[...] = (red[k, 0] + red[k, 1]) + (red[k, 2] + red[k, 3])
        yield

    sum_x = all_sum(0, x, xs)
    next(sum_x)
    next(rs1)
    next(rs0)
    next(sum_x)
    sum_y = all_sum(1, y, ys)
    next(sum_y)
    next(rs2)
    next(rs_u)
    mix_out[...] = (h2s[...] + rs_result(2)).astype(BF)
    next(rs0)
    next(sum_y)
    sum_z = all_sum(2, z, zs)
    next(sum_z)
    next(rs1)
    next(rs1)
    next(rs1)
    back1 = gather_grads(1)
    next(rs2)
    next(rs2)
    next(rs2)
    back2 = gather_grads(2)
    next(sum_z)
    red[3, core] = small_out[...]
    c = wire.send(red.at[3, core], red.at[3, core], peer)
    next(rs0)
    next(rs0)
    next(rs0)
    back0 = gather_grads(0)
    c.wait_recv()
    small_out[...] = red[3, 0] + red[3, 1]
    for copies, oa, out in ((back1, oa1, g1_out), (back2, oa2, g2_out), (back0, oa0, g0_out)):
        for c in copies:
            c.wait_recv()
        out[...] = oa[...].astype(F32)
    for gen in (ag0, ag1, ag2, ag_n1, ag_dy, ag_n2, ag_dh, rs0, rs1, rs2, rs_y, rs_n2, rs_u, rs_n1):
        assert next(gen, 0) == 0
    wire.finish()


def block(tokens, dy, code, vec, pack0, pack1, pack2):
    vmem = pl.BlockSpec(memory_space=pltpu.VMEM)
    plane = [pltpu.VMEM((4, 4, 64, w), BF) for w in WIDTHS]
    scratch = (
        plane
        + [pltpu.VMEM((4, 4, 64, w), BF) for w in WIDTHS]
        + [pltpu.VMEM((2, 6, 4, 16, w), BF) for w in WIDTHS]
        + [pltpu.VMEM((2, 6, 16, w), BF) for w in WIDTHS]
        + [pltpu.VMEM((4, 16, w), BF) for w in WIDTHS]
        + [
            pltpu.VMEM((4, TOK, CH), BF),
            pltpu.VMEM((GT, D), BF),
            pltpu.VMEM((GT, D), BF),
            pltpu.VMEM((GT, D), BF),
            pltpu.VMEM((GT, D), BF),
            pltpu.VMEM((4, GT, D), BF),
            pltpu.VMEM((4, GT, HALF), BF),
            pltpu.VMEM((4, GT, HALF), BF),
            pltpu.VMEM((4, 6, TOK // 2, HALF), BF),
            pltpu.VMEM((4, TOK, CH), F32),
            pltpu.VMEM((4, TOK, CH), F32),
            pltpu.VMEM((TOK, HALF), F32),
            pltpu.VMEM((TOK, HALF), F32),
            pltpu.VMEM((TOK, HALF), F32),
            pltpu.VMEM((TOK, HALF), F32),
            pltpu.VMEM((GT, 3 * CH), F32),
            pltpu.VMEM((GT, 3 * CH), BF),
            pltpu.VMEM((GT, CH), F32),
            pltpu.VMEM((GT, CH), BF),
            pltpu.VMEM((GT + 8, CH), F32),
            pltpu.VMEM((GT + 8, CH), F32),
            pltpu.VMEM((GT + 8, CH), F32),
            pltpu.VMEM((GT + 8, CH), F32),
            pltpu.VMEM((2, 2, 8, CH), F32),
            pltpu.VMEM((2, 2, 8, CH), F32),
            pltpu.VMEM((GT, HP), BF),
            pltpu.VMEM((GT, 2 * HP), BF),
            pltpu.VMEM((4, 4, 8, D), F32),
            pltpu.SemaphoreType.DMA((NCOPY,)),
            pltpu.SemaphoreType.DMA((NCOPY,)),
        ]
    )
    return pl.pallas_call(
        kernel,
        out_shape=[
            jax.ShapeDtypeStruct((TOK, HALF), BF),
            jax.ShapeDtypeStruct((TOK, HALF), F32),
            jax.ShapeDtypeStruct((8, D), F32),
        ]
        + [jax.ShapeDtypeStruct((4, 16, w), F32) for w in WIDTHS],
        in_specs=[vmem] * 7,
        out_specs=[vmem] * 6,
        scratch_shapes=scratch,
        compiler_params=pltpu.CompilerParams(
            collective_id=0, has_side_effects=True, vmem_limit_bytes=58 * 1024 * 1024
        ),
    )(tokens, dy, code, vec, pack0, pack1, pack2)


def local(
    tokens,
    segment_ids,
    valid_mask,
    norm1_gain,
    in_weight,
    conv_weight,
    out_weight,
    norm2_gain,
    gate_weight,
    up_weight,
    down_weight,
    out_cotangent,
):
    code = (segment_ids + 16 * valid_mask).astype(BF)
    code = jnp.broadcast_to(code[:, None], (TOK, CH))
    vec = jnp.concatenate(
        [norm1_gain[None], norm2_gain[None], conv_weight, jnp.zeros((3, D), BF)], axis=0
    ).astype(F32)

    def wide(w):
        return jnp.pad(w.reshape(16, 4, HID).transpose(1, 0, 2), ((0, 0), (0, 0), (0, HP - HID)))

    ins = in_weight.reshape(3, 16, 4, CH).transpose(2, 1, 0, 3).reshape(4, 16, 3 * CH)
    outs = out_weight.reshape(4, CH, 16).transpose(0, 2, 1)
    pack0 = jnp.concatenate([ins, outs], axis=2)
    pack1 = jnp.concatenate([wide(gate_weight), wide(up_weight)], axis=2)
    pack2 = jnp.pad(down_weight.reshape(4, HID, 16).transpose(0, 2, 1), ((0, 0), (0, 0), (0, HP - HID)))
    mixed, tokens_grad, small, p0, p1, p2 = block(tokens, out_cotangent, code, vec, pack0, pack1, pack2)
    grad_in = p0[:, :, : 3 * CH].reshape(4, 16, 3, CH).transpose(2, 1, 0, 3).reshape(3, 16, HALF)
    grad_out = p0[:, :, 3 * CH :].transpose(0, 2, 1).reshape(HALF, 16)
    grad_gate = p1[:, :, :HID].transpose(1, 0, 2).reshape(16, 4 * HID)
    grad_up = p1[:, :, HP : HP + HID].transpose(1, 0, 2).reshape(16, 4 * HID)
    grad_down = p2[:, :, :HID].transpose(0, 2, 1).reshape(4 * HID, 16)
    return (mixed, tokens_grad, small[0], grad_in, small[2:5], grad_out, small[1], grad_gate, grad_up, grad_down)


def solution(mesh):
    placed = (
        P("dp", "tensor"),
        P("dp"),
        P("dp"),
        P(),
        P(None, "dp", "tensor"),
        P(),
        P("tensor", "dp"),
        P(),
        P("dp", "tensor"),
        P("dp", "tensor"),
        P("tensor", "dp"),
        P("dp", "tensor"),
    )
    return jax.shard_map(
        local,
        mesh=mesh,
        in_specs=placed,
        out_specs=(
            P("dp", "tensor"),
            P("dp", "tensor"),
            P(),
            P(None, "dp", "tensor"),
            P(),
            P("tensor", "dp"),
            P(),
            P("dp", "tensor"),
            P("dp", "tensor"),
            P("tensor", "dp"),
        ),
        check_vma=False,
    )
```

time: 1890 us -> 146 us (0.08)
  waiting for transfers between devices: 1660 us -> 0 us
  Pallas kernels: 0 us -> 127 us
  blocking collectives: 87.2 us -> 0 us
  matrix products: 81.9 us -> 0 us
  other arithmetic: 23.4 us -> 2.69 us
    reduce_scatter x13 -> x0, waiting for transfers between devices: 1350 us -> none  [the longest x1 360 us: local(): lax.psum_scatter(grad_in, 'dp', scatter_dimension=1, tiled=True)]
    all_gather x5 -> x0, waiting for transfers between devices: 304 us -> none  [the longest x1 67.7 us: fetch_weights(): lax.all_gather(gate_weight, 'dp', axis=0, tiled=True)]
    pallas_call x0 -> x1, Pallas kernels: none -> 127 us  [block(): pl.pallas_call(kernel, out_shape=[jax.ShapeDtypeStruct((TOK, HALF), BF),...]
    dot_general x42 -> x0, matrix products: 81.9 us -> none  [the longest x2 9.25 us: local(): ffn_partial = jnp.dot(hidden, down_full, preferred_element_type=jnp.float32)]
    psum x1 -> x0, blocking collectives: 71.6 us -> none  [local(): lax.psum((conv_full, grad_gain_one, grad_gain_two), ('dp', 'tensor'))]
  transfers between devices with their start and end apart: 22 -> 0, of which waited for: 12 -> 0; matrix products, arithmetic and copies ran while one was open for 5% -> 0% of each run, Pallas kernels for 0% -> 0%
where the time goes in v1:
time: 146 us; the launch traced here: 145 us
  Pallas kernels  127 us (87%)
  local copies, waits for them, and re-layouts  14.4 us (10%)
  other arithmetic  2.69 us (2%)
    pallas_call x1, Pallas kernels, block(): pl.pallas_call(kernel, out_shape=[jax.ShapeDtypeStruct((TOK, HALF), BF),...  127 us
    unnamed x28, local copies, waits for them, and re-layouts  4.77 us

profile of v1, /device:TPU:0, one launch (start us, length us, event | category | flops | bytes accessed | tf_op | source)
XLA Modules:
  0.0 145.1 jit_solution(11874358646062031731)
XLA Ops:
  0.7 0.7 add_convert_fusion
  1.4 0.6 copy-done.11
  2.0 0.7 copy-done.12
  2.7 0.7 copy-done.10
  3.4 0.7 maximum_convert_fusion.vec_ref
  4.1 0.7 broadcast_in_dim.15.code_ref
  4.9 0.6 pad_maximum_fusion.pack0
  5.6 0.2 copy-done.6
  5.8 0.1 reshape.60
  6.0 0.7 copy-done.7
  6.9 0.7 fusion.2.pack1
  7.6 0.2 copy-done.8
  7.9 0.6 pad.12.pack2
  8.6 127.2 %shard_map.195 = (bf16[128,512]{1,0:T(8,128)(2,1)}, f32[128,512]{1,0:T(8,128)}, f32[8,1024]{1,0:T(8,128)}, f32[4,16,512]{2,1,0:T(8,128)}, f32[4,16,1280]{2,1,0:T(8,128)}, /*index=5*/f32[4,16,640]{2,1,0:T(8,128)}) custom-call(bf16[128,512]{1,0:T(8,128)(2,1)} %tok_ref.1, bf16[128,512]{1,0:T(8,128)(2,1)} %dy_ref.1, bf16[128,128]{1,0:T(8,128)(2,1)} %broadcast_in_dim.15.code_ref, ...), custom_call_target="tpu_custom_call" | custom-call | tf_op jit(solution)/shard_map/pallas_call | solution.py:606
  135.8 1.4 fusion.3
  137.2 1.4 slice.26
  138.6 1.4 copy_bitcast_fusion.4
  140.1 0.7 reshape.64
  140.8 0.2 copy-done.3
  141.1 0.8 reshape.68
  142.0 0.8 reshape.67
  142.9 0.8 reshape.66
  143.8 0.7 copy.55
  144.4 0.7 copy.56
  (39 shorter events, 1.0 us)
Async XLA Ops:
  0.6 2.1 %copy-start = (bf16[512,16]{0,1:T(8,128)(2,1)S(1)}, bf16[512,16]{0,1:T(8,128)(2,1)}, u32[]{:S(2)}) copy-start(bf16[512,16]{0,1:T(8,128)(2,1)} %param.18) | copy-start | bytes 49156
  1.3 0.7 copy-start.11
  2.0 0.7 copy-start.12
  2.7 0.7 copy-start.10
  3.4 1.4 copy-start.9
  4.9 0.9 copy-start.6
  5.8 0.9 copy-start.7
  6.9 0.9 copy-start.8
  135.8 4.2 %copy-start.4 = (f32[4,16,512]{2,1,0:T(8,128)S(1)}, f32[4,16,512]{2,1,0:T(8,128)}, u32[]{:S(2)}) copy-start(f32[4,16,512]{2,1,0:T(8,128)} %get-tuple-element.19) | copy-start | bytes 393220
  140.0 0.9 copy-start.3
  141.0 1.0 copy-start.1
  142.8 0.9 copy-start.5
  142.9 1.5 %copy-start.2 = (f32[128,512]{1,0:T(8,128)S(1)}, f32[128,512]{1,0:T(8,128)}, u32[]{:S(2)}) copy-start(f32[128,512]{1,0:T(8,128)} %get-tuple-element.39) | copy-start | bytes 786436

commit v2 on v1

v2 whole, which is shorter than its diff:
```python
import jax
import jax.numpy as jnp
from jax import lax
from jax.experimental import pallas as pl
from jax.experimental.pallas import tpu as pltpu
from jax.sharding import PartitionSpec as P

D = 1024
EPS = 1e-05
R = 4
BF = jnp.bfloat16
F32 = jnp.float32
TOK = 128
GT = 512
HALF = 512
CH = 128
HID = 576
HP = 640
WIDTHS = (512, 2 * HP, HP)
SENDS = 48
RECEIVES = 186


def nn(a, b):
    return lax.dot_general(a, b, (((1,), (0,)), ((), ())), preferred_element_type=F32)


def nt(a, b):
    return lax.dot_general(a, b, (((1,), (1,)), ((), ())), preferred_element_type=F32)


def tn(a, b):
    return lax.dot_general(a, b, (((0,), (0,)), ((), ())), preferred_element_type=F32)


def add_into(dst, *others):
    total = dst[...].astype(F32)
    for other in others:
        total = total + other[...].astype(F32)
    dst[...] = total.astype(dst.dtype)


class Event:
    def __init__(self):
        self.time = float("inf")


class Copy(Event):
    def __init__(self, copy, time, end):
        self.copy, self.time, self.end, self.waited = copy, time, end, False


class Group(Event):
    def __init__(self, total):
        self.total, self.sem, self.time, self.waited = total, None, 0.0, False


class Room:
    def __init__(self, schedule, link, slack):
        self.schedule, self.link, self.slack = schedule, link, slack

    @property
    def time(self):
        return self.schedule.free.get(self.link, 0.0) - self.slack


class Schedule:
    RATE = 46.8e3
    CORE_RATE = 700e3
    LATENCY = 1.65
    FAR_LATENCY = 2.3
    CORE_LATENCY = 0.9
    ISSUE = 0.05

    def __init__(self, send_sems, recv_sems):
        self.send_sems, self.recv_sems = send_sems, recv_sems
        self.pool, self.received = [None] * SENDS, 0
        self.tasks, self.free, self.now = [], {}, 2.0

    def send(self, src, dst, device, *links, group=None):
        k = min(range(SENDS), key=lambda i: -1.0 if self.pool[i] is None else self.pool[i].end)
        if self.pool[k] is not None:
            self.pool[k].copy.wait_send()
            self.now = max(self.now, self.pool[k].end)
        sem = self.received if group is None or group.sem is None else group.sem
        if sem == self.received:
            self.received += 1
            assert sem < RECEIVES
        copy = pltpu.make_async_remote_copy(
            src_ref=src,
            dst_ref=dst,
            send_sem=self.send_sems.at[k],
            recv_sem=self.recv_sems.at[sem],
            device_id=device,
            device_id_type=pl.DeviceIdType.MESH,
        )
        copy.start()
        self.now += self.ISSUE
        size = jnp.dtype(src.dtype).itemsize
        for n in src.shape:
            size *= n
        end = self.now
        for link in links:
            begin = max(self.now, self.free.get(link, 0.0))
            self.free[link] = begin + size / (self.CORE_RATE if link == "c" else self.RATE)
            end = max(end, self.free[link])
        latency = self.CORE_LATENCY if "c" in links else self.LATENCY if len(links) == 1 else self.FAR_LATENCY
        self.pool[k] = Copy(copy, end + latency, end)
        if group is None:
            return self.pool[k]
        group.sem, group.time = sem, max(group.time, end + latency)
        group.copy = pltpu.make_async_remote_copy(
            src_ref=group.total,
            dst_ref=group.total,
            send_sem=self.send_sems.at[k],
            recv_sem=self.recv_sems.at[sem],
            device_id=device,
            device_id_type=pl.DeviceIdType.MESH,
        )
        return group

    def room(self, link, slack=0.8):
        return [Room(self, link, slack)]

    def work(self, us):
        self.now += us

    def done(self, event):
        event.time = self.now

    def add(self, rank, task):
        self.tasks.append([rank, task, ()])

    def run(self):
        while self.tasks:
            times = [max([0.0] + [e.time for e in t[2]]) for t in self.tasks]
            ready = [i for i, r in enumerate(times) if r <= self.now]
            if ready:
                i = min(ready, key=lambda i: (self.tasks[i][0], times[i]))
            else:
                i = min(range(len(times)), key=lambda i: (times[i], self.tasks[i][0]))
                self.now = times[i]
            task = self.tasks[i]
            for event in task[2]:
                if isinstance(event, (Copy, Group)) and not event.waited:
                    event.copy.wait_recv()
                    event.waited = True
                    self.now += 0.03
            try:
                task[2] = tuple(next(task[1]))
            except StopIteration:
                self.tasks.pop(i)
        for last in self.pool:
            if last is not None:
                last.copy.wait_send()


def ring_ag(s, axis, i, plus, minus, blk, two, issued=None):
    rest = Group(two)
    up, down = axis + "+", axis + "-"
    prev, nxt = (i + R - 1) % R, (i + 1) % R
    yield s.room(up)
    c1 = s.send(blk(i, 0), blk(i, 0), plus, up)
    yield s.room(down)
    c2 = s.send(blk(i, 1), blk(i, 1), minus, down)
    yield s.room(up)
    s.send(blk(i, 1), blk(i, 1), plus, up, group=rest)
    yield s.room(down)
    s.send(blk(i, 0), blk(i, 0), minus, down, group=rest)
    yield [c1]
    s.send(blk(prev, 0), blk(prev, 0), plus, up, group=rest)
    yield [c2]
    s.send(blk(nxt, 1), blk(nxt, 1), minus, down, group=rest)
    if issued is not None:
        s.done(issued)
    yield [rest]


def ring_rs(s, axis, i, plus, minus, blk, bufs, us):
    recv, rest = [bufs.at[k] for k in range(6)], Group(bufs.at[pl.ds(2, 4)])
    up, down = axis + "+", axis + "-"
    prev, nxt, far = (i + R - 1) % R, (i + 1) % R, (i + 2) % R
    yield s.room(up)
    c1 = s.send(blk(far, 0), recv[0], plus, up)
    yield s.room(down)
    c2 = s.send(blk(far, 1), recv[1], minus, down)
    yield s.room(up)
    s.send(blk(nxt, 1), recv[2], plus, up, group=rest)
    yield s.room(down)
    s.send(blk(prev, 0), recv[3], minus, down, group=rest)
    yield [c1]
    add_into(blk(nxt, 0), recv[0])
    s.work(us)
    s.send(blk(nxt, 0), recv[4], plus, up, group=rest)
    yield [c2]
    add_into(blk(prev, 1), recv[1])
    s.work(us)
    s.send(blk(prev, 1), recv[5], minus, down, group=rest)
    yield [rest]


def kernel(
    tok_ref,
    dy_ref,
    code_ref,
    vec_ref,
    pack0,
    pack1,
    pack2,
    mix_out,
    tg_out,
    small_out,
    g0_out,
    g1_out,
    g2_out,
    w0,
    w1,
    w2,
    g0,
    g1,
    g2,
    ra0,
    ra1,
    ra2,
    ra3,
    rb0,
    rb1,
    rb2,
    rb3,
    oa0,
    oa1,
    oa2,
    codes,
    tail_raw,
    tail_code,
    tail_s,
    tail_r,
    tail,
    n1,
    dyf,
    n2,
    dhb,
    zpart,
    zrc,
    zp,
    zr,
    zd,
    stat_s,
    stat_r,
    hat1,
    hat2,
    h2s,
    dh2s,
    bcv,
    dbcv,
    zc,
    gat,
    mx,
    cd,
    q0,
    q1,
    q2,
    halo_s,
    halo_r,
    uu,
    dab,
    red,
    send_sems,
    recv_sems,
):
    dp = lax.axis_index("dp")
    core = lax.axis_index("tensor")
    y, x, z = dp // 16, (dp // 4) % 4, dp % 4
    group = dp // 4

    def dev(yy, xx, zz):
        return (yy * 16 + xx * 4 + zz, core)

    def up(v, k=1):
        return (v + k) % R

    peer = (dp, 1 - core)
    xs = [None] + [dev(y, up(x, k), z) for k in (1, 2, 3)]
    ys = [None] + [dev(up(y, k), x, z) for k in (1, 2, 3)]
    zs = [None] + [dev(y, x, up(z, k)) for k in (1, 2, 3)]
    after = ((dp + 4) % 64, core)
    before = ((dp + 60) % 64, core)

    barrier = pltpu.get_barrier_semaphore()
    others = [peer, after, before] + xs[1:] + ys[1:] + zs[1:]
    for other in others:
        pl.semaphore_signal(barrier, inc=1, device_id=other, device_id_type=pl.DeviceIdType.MESH)
    pl.semaphore_wait(barrier, len(others))

    s = Schedule(send_sems, recv_sems)
    packs, ws, gs = (pack0, pack1, pack1, pack2), (w0, w1, w1, w2), (g0, g1, g1, g2)
    ras, rbs, oas = (ra0, ra1, ra2, ra3), (rb0, rb1, rb2, rb3), (oa0, oa1, oa1, oa2)
    outs = (g0_out, g1_out, g1_out, g2_out)
    lanes = (pl.ds(0, 512), pl.ds(0, HP), pl.ds(HP, HP), pl.ds(0, HP))
    my_cols = pl.ds(pl.multiple_of(core * HALF, HALF), HALF)
    peer_cols = pl.ds(pl.multiple_of((1 - core) * HALF, HALF), HALF)
    ch_cols = pl.ds(pl.multiple_of(core * HALF + z * CH, CH), CH)
    z_links = (None, ("z+",), ("z+", "z-"), ("z-",))
    links = {a: (None, (a + "+",), (a + "+", a + "-"), (a + "-",)) for a in "xyz"}

    def rows_of(j, count=TOK):
        return pl.ds(pl.multiple_of(j * count, count), count)

    def ag_plane(c, issued):
        w, ln = ws[c], lanes[c]

        def part(base, h):
            return pl.ds(base + 16 * h, 16)

        def side_a():
            yield from ring_ag(s, "x", x, xs[1], xs[3], lambda j, h: w.at[y, j, part(0, h), ln], w.at[y, x, :, ln])
            if c:
                yield [issued[c - 1][0]]
            yield from ring_ag(s, "y", y, ys[1], ys[3], lambda j, h: w.at[j, :, part(0, h), ln], w.at[y, :, :, ln], issued[c][0])

        def side_b():
            yield from ring_ag(s, "y", y, ys[1], ys[3], lambda j, h: w.at[j, x, part(32, h), ln], w.at[y, x, :, ln])
            if c:
                yield [issued[c - 1][1]]
            yield from ring_ag(s, "x", x, xs[1], xs[3], lambda j, h: w.at[:, j, part(32, h), ln], w.at[:, x, :, ln], issued[c][1])

        return side_a, side_b

    def rs_plane(c):
        g, ra, rb, ln, us = gs[c], ras[c], rbs[c], lanes[c], 0.12

        def part(base, h):
            return pl.ds(base + 16 * h, 16)

        def side_a():
            yield from ring_rs(
                s, "y", y, ys[1], ys[3], lambda j, h: g.at[j, :, part(0, h), ln], ra.at[0], us
            )
            for h, (u, v) in ((0, (3, 4)), (1, (2, 5))):
                add_into(g.at[y, :, part(0, h), ln], ra.at[0, u], ra.at[0, v])
                s.work(1.5 * us)
            yield from ring_rs(
                s, "x", x, xs[1], xs[3], lambda j, h: g.at[y, j, part(0, h), ln], rb.at[0], us / 3
            )
            for h, (u, v) in ((0, (3, 4)), (1, (2, 5))):
                add_into(g.at[y, x, part(0, h), ln], rb.at[0, u], rb.at[0, v])
                s.work(0.5 * us)

        def side_b():
            yield from ring_rs(
                s, "x", x, xs[1], xs[3], lambda j, h: g.at[:, j, part(32, h), ln], ra.at[1], us
            )
            for h, (u, v) in ((0, (3, 4)), (1, (2, 5))):
                add_into(g.at[:, x, part(32, h), ln], ra.at[1, u], ra.at[1, v])
                s.work(1.5 * us)
            yield from ring_rs(
                s, "y", y, ys[1], ys[3], lambda j, h: g.at[j, x, part(32, h), ln], rb.at[1], us / 3
            )
            for h, (u, v) in ((0, (3, 4)), (1, (2, 5))):
                add_into(g.at[y, x, part(32, h), ln], rb.at[1, u], rb.at[1, v])
                s.work(0.5 * us)

        return side_a, side_b

    prev, nxt, far = up(z, 3), up(z), up(z, 2)

    def ag_group(n, have, issued):
        def both(j, h, device, link, group=None):
            ref = n.at[half_rows(j, h), my_cols]
            return s.send(ref, ref, device, link, group=group)

        to_core = [Group(n.at[rows_of(j), my_cols]) for j in (z, prev, nxt, far)]

        def core_too(i, j, h):
            both(j, h, peer, "c", to_core[i])

        c1 = both(z, 0, zs[1], "z+")
        c2 = both(z, 1, zs[3], "z-")
        c3 = both(z, 1, zs[1], "z+")
        c4 = both(z, 0, zs[3], "z-")
        core_too(0, z, 0)
        core_too(0, z, 1)
        yield [to_core[0]]
        s.done(have[0])
        yield [c1]
        c5 = both(prev, 0, zs[1], "z+")
        core_too(1, prev, 0)
        yield [c2]
        c6 = both(nxt, 1, zs[3], "z-")
        s.done(issued)
        core_too(2, nxt, 1)
        yield [c3]
        core_too(1, prev, 1)
        yield [c4]
        core_too(2, nxt, 0)
        yield [to_core[1]]
        s.done(have[1])
        yield [to_core[2]]
        s.done(have[2])
        yield [c5]
        core_too(3, far, 0)
        yield [c6]
        core_too(3, far, 1)
        yield [to_core[3]]
        s.done(have[3])

    def half_rows(j, h):
        return pl.ds(pl.multiple_of(j * TOK + h * (TOK // 2), TOK // 2), TOK // 2)

    def share_core(k, j):
        return s.send(zpart.at[k, rows_of(j), peer_cols], zrc.at[k, rows_of(j)], peer, "c")

    def add_core(k, j):
        rows = rows_of(j)
        zp[k, rows] = (zpart[k, rows, my_cols].astype(F32) + zrc[k, rows].astype(F32)).astype(BF)
        s.work(0.15)

    def rs_group(k, part):
        def blk(j, h):
            return zp.at[k, half_rows(j, h)]

        recv = [zr.at[k, i] for i in range(6)]
        rest = Group(zr.at[k, pl.ds(2, 4)])
        order = (far, nxt, prev, z)
        copies = []
        for j in order:
            part(j)
            copies.append(share_core(k, j))
            yield []
        yield [copies[0]]
        add_core(k, far)
        c1 = s.send(blk(far, 0), recv[0], zs[1], "z+")
        c2 = s.send(blk(far, 1), recv[1], zs[3], "z-")
        yield [copies[1]]
        add_core(k, nxt)
        s.send(blk(nxt, 1), recv[2], zs[1], "z+", group=rest)
        yield [copies[2]]
        add_core(k, prev)
        s.send(blk(prev, 0), recv[3], zs[3], "z-", group=rest)
        yield [c1]
        add_into(blk(nxt, 0), recv[0])
        s.work(0.06)
        s.send(blk(nxt, 0), recv[4], zs[1], "z+", group=rest)
        yield [c2]
        add_into(blk(prev, 1), recv[1])
        s.work(0.06)
        s.send(blk(prev, 1), recv[5], zs[3], "z-", group=rest)
        yield [copies[3]]
        add_core(k, z)
        yield [rest]

    def rs_result(k):
        if k == 1:
            total = zp[k, rows_of(z)].astype(F32)
            for h in range(3):
                total = total + zd[h].astype(F32)
            return total

        def half(h, u, v):
            return zp[k, half_rows(z, h)].astype(F32) + zr[k, u].astype(F32) + zr[k, v].astype(F32)

        return jnp.concatenate([half(0, 3, 4), half(1, 2, 5)], axis=0)

    def chip_sum(k, values):
        stat_s[k] = jnp.broadcast_to(jnp.sum(values, axis=1, keepdims=True), (TOK, CH))
        return s.send(stat_s.at[k], stat_r.at[k], peer, "c")

    def chip_total(k):
        return (stat_s[k] + stat_r[k])[:, :1]

    def events(*dims):
        return [events(*dims[1:]) for _ in range(dims[0])] if dims else Event()

    dealt, full_w, issued = events(4), events(4, 2), events(4, 2)
    have_n1, have_n2, have_dy, have_dh = events(4), events(4), events(4), events(4)
    sent_n1, sent_n2, sent_dy, sent_dh = events(4)
    have_codes, have_halo, ffn, conv_back, sums = events(5)
    gain1 = vec_ref[pl.ds(0, 1), my_cols]
    gain2 = vec_ref[pl.ds(1, 1), my_cols]
    taps = [vec_ref[pl.ds(2 + k, 1), ch_cols] for k in range(3)]

    def deal(c):
        mine = pl.ds(pl.multiple_of(z * 16, 16), 16)
        slab = ws[c].at[y, x, mine, lanes[c]]
        group = Group(ws[c].at[y, x, pl.ds(0, 48), lanes[c]])
        for k in (1, 3, 2):
            s.send(packs[c].at[up(z, k), :, lanes[c]], slab, zs[k], *z_links[k], group=group)
        ws[c][y, x, mine, lanes[c]] = packs[c][z, :, lanes[c]]
        s.work(0.1)
        yield [group]
        s.done(dealt[c])

    def gather_side(c, h, side):
        yield [dealt[c]]
        yield from side()
        s.done(full_w[c][h])

    def first_norm():
        tok = tok_ref[...].astype(F32)
        copy = chip_sum(0, tok * tok)
        s.work(0.3)
        yield [copy]
        r1 = lax.rsqrt(chip_total(0) * (1.0 / D) + EPS)
        hat1[...] = tok_ref[...].astype(F32) * r1
        n1[rows_of(z), my_cols] = (hat1[...] * gain1).astype(BF)
        s.work(0.3)
        yield from ag_group(n1, have_n1, sent_n1)

    def halo():
        yield [
            s.send(tok_ref.at[pl.ds(TOK - 16, 16)], tail_raw, after, "x+"),
            s.send(code_ref, tail_code.at[z], after, "x+"),
        ]
        tok = tail_raw[...].astype(F32)
        tail_s[...] = jnp.broadcast_to(jnp.sum(tok * tok, axis=1, keepdims=True), (16, CH))
        yield [s.send(tail_s, tail_r, peer, "c")]
        scale = lax.rsqrt((tail_s[...] + tail_r[...])[:, :1] * (1.0 / D) + EPS)
        tail[z, :, my_cols] = (tail_raw[...].astype(F32) * scale * gain1).astype(BF)
        ref = tail.at[z, :, my_cols]
        group1, group2 = Group(tail.at[pl.ds(0, 3), :, my_cols]), Group(tail_code.at[pl.ds(0, 3)])
        for k in (1, 3, 2):
            s.send(ref, ref, zs[k], *z_links[k], group=group1)
            s.send(tail_code.at[z], tail_code.at[z], zs[k], *z_links[k], group=group2)
        s.work(0.1)
        yield [group1, group2]
        ref = tail.at[3, :, my_cols]
        yield [s.send(ref, ref, peer, "c")]
        n1[pl.ds(GT, 16), :] = tail[3]
        s.done(have_halo)

    def column(row):
        return jnp.transpose(jnp.broadcast_to(row, (CH, CH)))

    def share_codes():
        codes[z] = code_ref[...]
        group = Group(codes.at[pl.ds(0, 3)])
        for k in (1, 3, 2):
            s.send(code_ref, codes.at[z], zs[k], *z_links[k], group=group)
        yield [group]
        for j in range(4):
            cd[pl.ds(8 + j * TOK, TOK), :] = column(codes[j, 0:1])
        s.work(0.4)
        yield [have_halo]
        before_code = column(tail_code[3, 0:1])[TOK - 8 :]
        cd[pl.ds(0, 8), :] = jnp.where(group == 0, -1.0, before_code)
        s.work(0.1)
        s.done(have_codes)

    def share_dy():
        yield [sent_n1]
        dyf[rows_of(z), my_cols] = dy_ref[...]
        s.work(0.1)
        yield from ag_group(dyf, have_dy, sent_dy)

    def keep(k):
        code = cd[pl.ds(8, GT), :]
        return jnp.where((code >= 16.0) & (code == cd[pl.ds(8 - k, GT), :]), 1.0, 0.0)

    def ffn_block(j):
        rows = rows_of(j)
        ab = nn(n2[rows, :], w1[...].reshape(D, 2 * HP))
        a, b = ab[:, :HP], ab[:, HP:]
        sg = jax.nn.sigmoid(a)
        silu = a * sg
        uu[rows, :] = (silu * b).astype(BF)
        du = nn(dyf[rows, :], w2[...].reshape(D, HP))
        dab[rows, 0:HP] = (du * b * sg * (1.0 + a * (1.0 - sg))).astype(BF)
        dab[rows, HP : 2 * HP] = (du * silu).astype(BF)
        s.work(1.0)

    def y_part(j):
        rows = rows_of(j)
        zpart[0, rows, :] = nt(gat[rows, :], w0[...].reshape(D, 512)[:, 3 * CH :]).astype(BF)
        s.work(0.15)

    def n2_part(j):
        rows = rows_of(j)
        zpart[1, rows, :] = nt(dab[rows, :], w1[...].reshape(D, 2 * HP)).astype(BF)
        s.work(0.6)

    def u_part(j):
        rows = rows_of(j)
        zpart[2, rows, :] = nt(uu[rows, :], w2[...].reshape(D, HP)).astype(BF)
        s.work(0.35)

    def n1_part(j):
        rows = rows_of(j)
        zpart[3, rows, :] = nt(dbcv[rows, :], w0[...].reshape(D, 512)[:, : 3 * CH]).astype(BF)
        s.work(0.25)

    def main():
        yield have_n1 + full_w[0] + [have_halo]
        bcv[...] = nn(n1[...], w0[...].reshape(D, 512)[:, : 3 * CH])
        mixed = (bcv[:, 0:CH] * bcv[:, 2 * CH : 3 * CH]).astype(BF).astype(F32)
        mx[pl.ds(8, GT), :] = mixed[:GT]
        mx[pl.ds(0, 8), :] = mixed[GT + 8 :]
        s.work(1.0)
        yield [have_codes]
        zc[...] = (
            taps[0] * mx[pl.ds(8, GT), :] * keep(0)
            + taps[1] * mx[pl.ds(7, GT), :] * keep(1)
            + taps[2] * mx[pl.ds(6, GT), :] * keep(2)
        )
        gat[...] = (bcv[pl.ds(0, GT), CH : 2 * CH] * zc[...]).astype(BF)
        s.work(0.4)
        yield from rs_group(0, y_part)
        h2s[...] = tok_ref[...].astype(F32) + rs_result(0)
        h2 = h2s[...]
        copy = chip_sum(1, h2 * h2)
        s.work(0.4)
        yield [copy]
        r2 = lax.rsqrt(chip_total(1) * (1.0 / D) + EPS)
        hat2[...] = h2s[...] * r2
        n2[rows_of(z), my_cols] = (hat2[...] * gain2).astype(BF)
        s.work(0.3)
        s.add(1, ag_group(n2, have_n2, sent_n2))
        yield have_dy + full_w[1] + full_w[2] + full_w[3]
        last = Group(zd)
        for j, event, copy in ((z, have_n2[0], 0), (prev, have_n2[1], 3), (nxt, have_n2[2], 1), (far, have_n2[3], 2)):
            yield [event]
            ffn_block(j)
            if copy == 2:
                s.done(ffn)
            yield []
            n2_part(j)
            shared = share_core(1, j)
            s.add(1, send_block(j, copy, shared, last))
            yield []
        yield block_sent
        yield [last]
        dn2 = rs_result(1)
        small_out[...] = jnp.zeros((8, D), F32)
        small_out[pl.ds(1, 1), my_cols] = jnp.sum(dn2 * hat2[...], axis=0, keepdims=True)
        e2 = dn2 * gain2
        copy = chip_sum(2, e2 * hat2[...])
        s.work(0.4)
        yield [copy]
        m2 = chip_total(2) * (1.0 / D)
        r2 = lax.rsqrt(chip_total(1) * (1.0 / D) + EPS)
        e2 = rs_result(1) * gain2
        dh2s[...] = dy_ref[...].astype(F32) + r2 * (e2 - hat2[...] * m2)
        dhb[rows_of(z), my_cols] = dh2s[...].astype(BF)
        s.work(0.4)
        yield from ag_group(dhb, have_dh, sent_dh)

        dg = nn(dhb[...], w0[...].reshape(D, 512)[:, 3 * CH :])
        dbcv[:, CH : 2 * CH] = (dg * zc[...]).astype(BF)
        dz = dg * bcv[pl.ds(0, GT), CH : 2 * CH]
        q0[...] = dz * keep(0)
        q1[pl.ds(0, GT), :] = dz * keep(1)
        q2[pl.ds(0, GT), :] = dz * keep(2)
        halo_s[0] = q1[pl.ds(0, 8), :]
        halo_s[1] = q2[pl.ds(0, 8), :]
        s.work(0.6)
        copy = s.send(halo_s, halo_r, before, "x-")
        small_out[pl.ds(2, 1), ch_cols] = jnp.sum(q0[...] * mx[pl.ds(8, GT), :], axis=0, keepdims=True)
        small_out[pl.ds(3, 1), ch_cols] = jnp.sum(q1[pl.ds(0, GT), :] * mx[pl.ds(7, GT), :], axis=0, keepdims=True)
        small_out[pl.ds(4, 1), ch_cols] = jnp.sum(q2[pl.ds(0, GT), :] * mx[pl.ds(6, GT), :], axis=0, keepdims=True)
        s.work(0.3)
        yield [copy]
        last = group == 15
        q1[pl.ds(GT, 8), :] = jnp.where(last, 0.0, halo_r[0])
        q2[pl.ds(GT, 8), :] = jnp.where(last, 0.0, halo_r[1])
        dm = taps[0] * q0[...] + taps[1] * q1[pl.ds(1, GT), :] + taps[2] * q2[pl.ds(2, GT), :]
        dbcv[:, 0:CH] = (dm * bcv[pl.ds(0, GT), 2 * CH : 3 * CH]).astype(BF)
        dbcv[:, 2 * CH : 3 * CH] = (dm * bcv[pl.ds(0, GT), 0:CH]).astype(BF)
        s.work(0.4)
        s.done(conv_back)
        yield []

        yield from rs_group(3, n1_part)
        dn1 = rs_result(3)
        small_out[pl.ds(0, 1), my_cols] = jnp.sum(dn1 * hat1[...], axis=0, keepdims=True)
        e1 = dn1 * gain1
        copy = chip_sum(3, e1 * hat1[...])
        s.work(0.4)
        s.done(sums)
        yield [copy]
        m1 = chip_total(3) * (1.0 / D)
        r1 = lax.rsqrt(chip_total(0) * (1.0 / D) + EPS)
        e1 = rs_result(3) * gain1
        tg_out[...] = dh2s[...] + r1 * (e1 - hat1[...] * m1)
        s.work(0.4)

    def small_sums():
        yield [sums]
        for k, (axis, i, peers) in enumerate((("x", x, xs), ("y", y, ys), ("z", z, zs))):
            red[k, i] = small_out[...]
            group = Group(red.at[k, pl.ds(0, 3)])
            for j in (1, 3, 2):
                s.send(red.at[k, i], red.at[k, i], peers[j], *links[axis][j], group=group)
            yield [group]
            small_out[...] = (red[k, 0] + red[k, 1]) + (red[k, 2] + red[k, 3])
            s.work(0.1)
        red[3, core] = small_out[...]
        yield [s.send(red.at[3, core], red.at[3, core], peer, "c")]
        small_out[...] = red[3, 0] + red[3, 1]

    block_sent = events(4)

    def send_block(j, k, shared, last):
        yield [shared]
        add_core(1, j)
        if k:
            s.send(zp.at[1, rows_of(j)], zd.at[k - 1], zs[k], *z_links[k], group=last)
        s.done(block_sent[k])

    def hidden_out():
        yield [sent_dh]
        yield from rs_group(2, u_part)
        mix_out[...] = (h2s[...] + rs_result(2)).astype(BF)
        s.work(0.2)

    def make_half(h):
        def step(i):
            ln = lanes[1 + h]
            g1[i, :, :, ln] = tn(n2[:, pl.ds(i * 256, 256)], dab[:, ln]).astype(BF).reshape(4, 64, HP)
            s.work(0.4)

        return step

    def make_g2(i):
        g2[i] = tn(dyf[:, pl.ds(i * 256, 256)], uu[...]).astype(BF).reshape(4, 64, HP)
        s.work(0.4)

    def make_g0(i):
        cols = pl.ds(i * 256, 256)
        g0[i, :, :, 0 : 3 * CH] = tn(n1[pl.ds(0, GT), cols], dbcv[...]).astype(BF).reshape(4, 64, 3 * CH)
        g0[i, :, :, 3 * CH : 4 * CH] = tn(dhb[:, cols], gat[...]).astype(BF).reshape(4, 64, CH)
        s.work(0.35)

    made, summed = events(4), events(4, 2)

    def make(c, after_event, step):
        yield [after_event]
        for i in range(4):
            step(i)
            yield []
        s.done(made[c])

    def reduce_side(c, h, side):
        yield [made[c]]
        yield from side()
        s.done(summed[c][h])

    def hand_back(c):
        yield summed[c]
        ln = lanes[c]

        def rows(j):
            return gs[c].at[y, x, pl.ds(pl.multiple_of(j * 16, 16), 16), ln]

        group = Group(oas[c].at[pl.ds(0, 3), :, ln])
        for k in (1, 3, 2):
            s.send(rows(up(z, k)), oas[c].at[z, :, ln], zs[k], *z_links[k], group=group)
        oas[c][z, :, ln] = rows(z)[...]
        yield [group]
        outs[c][:, :, ln] = oas[c][:, :, ln].astype(F32)
        s.work(0.2)

    s.add(0, halo())
    s.add(0, deal(0))
    s.add(1, first_norm())
    for c in (1, 2, 3):
        s.add(1 + c, deal(c))
    s.add(4, share_codes())
    s.add(6, share_dy())
    for c in range(4):
        for h, side in enumerate(ag_plane(c, issued)):
            s.add(2 + c, gather_side(c, h, side))
    s.add(7, main())
    for c, after_event, step in ((1, ffn, make_half(0)), (2, ffn, make_half(1)), (3, ffn, make_g2), (0, conv_back, make_g0)):
        s.add(8 + c, make(c, after_event, step))
        for h, side in enumerate(rs_plane(c)):
            s.add(2 + c, reduce_side(c, h, side))
        s.add(4, hand_back(c))
    s.add(13, hidden_out())
    s.add(2, small_sums())
    s.run()


def block(tokens, dy, code, vec, pack0, pack1, pack2):
    vmem = pl.BlockSpec(memory_space=pltpu.VMEM)
    plane = [pltpu.VMEM((4, 4, 64, w), BF) for w in WIDTHS]
    scratch = (
        plane
        + [pltpu.VMEM((4, 4, 64, w), BF) for w in WIDTHS]
        + [pltpu.VMEM((2, 6, 4, 16, w), BF) for w in (512, HP, HP, HP)]
        + [pltpu.VMEM((2, 6, 16, w), BF) for w in (512, HP, HP, HP)]
        + [pltpu.VMEM((4, 16, w), BF) for w in WIDTHS]
        + [
            pltpu.VMEM((4, 8, CH), F32),
            pltpu.VMEM((16, HALF), BF),
            pltpu.VMEM((4, 8, CH), F32),
            pltpu.VMEM((16, CH), F32),
            pltpu.VMEM((16, CH), F32),
            pltpu.VMEM((4, 16, D), BF),
            pltpu.VMEM((GT + 16, D), BF),
            pltpu.VMEM((GT, D), BF),
            pltpu.VMEM((GT, D), BF),
            pltpu.VMEM((GT, D), BF),
            pltpu.VMEM((4, GT, D), BF),
            pltpu.VMEM((4, GT, HALF), BF),
            pltpu.VMEM((4, GT, HALF), BF),
            pltpu.VMEM((4, 6, TOK // 2, HALF), BF),
            pltpu.VMEM((3, TOK, HALF), BF),
            pltpu.VMEM((4, TOK, CH), F32),
            pltpu.VMEM((4, TOK, CH), F32),
            pltpu.VMEM((TOK, HALF), F32),
            pltpu.VMEM((TOK, HALF), F32),
            pltpu.VMEM((TOK, HALF), F32),
            pltpu.VMEM((TOK, HALF), F32),
            pltpu.VMEM((GT + 16, 3 * CH), F32),
            pltpu.VMEM((GT, 3 * CH), BF),
            pltpu.VMEM((GT, CH), F32),
            pltpu.VMEM((GT, CH), BF),
            pltpu.VMEM((GT + 8, CH), F32),
            pltpu.VMEM((GT + 8, CH), F32),
            pltpu.VMEM((GT, CH), F32),
            pltpu.VMEM((GT + 8, CH), F32),
            pltpu.VMEM((GT + 8, CH), F32),
            pltpu.VMEM((2, 8, CH), F32),
            pltpu.VMEM((2, 8, CH), F32),
            pltpu.VMEM((GT, HP), BF),
            pltpu.VMEM((GT, 2 * HP), BF),
            pltpu.VMEM((4, 4, 8, D), F32),
            pltpu.SemaphoreType.DMA((SENDS,)),
            pltpu.SemaphoreType.DMA((RECEIVES,)),
        ]
    )
    return pl.pallas_call(
        kernel,
        out_shape=[
            jax.ShapeDtypeStruct((TOK, HALF), BF),
            jax.ShapeDtypeStruct((TOK, HALF), F32),
            jax.ShapeDtypeStruct((8, D), F32),
        ]
        + [jax.ShapeDtypeStruct((4, 16, w), F32) for w in WIDTHS],
        in_specs=[vmem] * 7,
        out_specs=[vmem] * 6,
        scratch_shapes=scratch,
        compiler_params=pltpu.CompilerParams(
            collective_id=0, has_side_effects=True, vmem_limit_bytes=58 * 1024 * 1024
        ),
    )(tokens, dy, code, vec, pack0, pack1, pack2)


def local(
    tokens,
    segment_ids,
    valid_mask,
    norm1_gain,
    in_weight,
    conv_weight,
    out_weight,
    norm2_gain,
    gate_weight,
    up_weight,
    down_weight,
    out_cotangent,
):
    code = (segment_ids + 16 * valid_mask).astype(F32)
    code = jnp.broadcast_to(code[None], (8, CH))
    vec = jnp.concatenate(
        [norm1_gain[None], norm2_gain[None], conv_weight, jnp.zeros((3, D), BF)], axis=0
    ).astype(F32)

    def wide(w):
        return jnp.pad(w.reshape(16, 4, HID).transpose(1, 0, 2), ((0, 0), (0, 0), (0, HP - HID)))

    ins = in_weight.reshape(3, 16, 4, CH).transpose(2, 1, 0, 3).reshape(4, 16, 3 * CH)
    outs = out_weight.reshape(4, CH, 16).transpose(0, 2, 1)
    pack0 = jnp.concatenate([ins, outs], axis=2)
    pack1 = jnp.concatenate([wide(gate_weight), wide(up_weight)], axis=2)
    pack2 = jnp.pad(down_weight.reshape(4, HID, 16).transpose(0, 2, 1), ((0, 0), (0, 0), (0, HP - HID)))
    mixed, tokens_grad, small, p0, p1, p2 = block(tokens, out_cotangent, code, vec, pack0, pack1, pack2)
    grad_in = p0[:, :, : 3 * CH].reshape(4, 16, 3, CH).transpose(2, 1, 0, 3).reshape(3, 16, HALF)
    grad_out = p0[:, :, 3 * CH :].transpose(0, 2, 1).reshape(HALF, 16)
    grad_gate = p1[:, :, :HID].transpose(1, 0, 2).reshape(16, 4 * HID)
    grad_up = p1[:, :, HP : HP + HID].transpose(1, 0, 2).reshape(16, 4 * HID)
    grad_down = p2[:, :, :HID].transpose(0, 2, 1).reshape(4 * HID, 16)
    return (mixed, tokens_grad, small[0], grad_in, small[2:5], grad_out, small[1], grad_gate, grad_up, grad_down)


def solution(mesh):
    placed = (
        P("dp", "tensor"),
        P("dp"),
        P("dp"),
        P(),
        P(None, "dp", "tensor"),
        P(),
        P("tensor", "dp"),
        P(),
        P("dp", "tensor"),
        P("dp", "tensor"),
        P("tensor", "dp"),
        P("dp", "tensor"),
    )
    return jax.shard_map(
        local,
        mesh=mesh,
        in_specs=placed,
        out_specs=(
            P("dp", "tensor"),
            P("dp", "tensor"),
            P(),
            P(None, "dp", "tensor"),
            P(),
            P("tensor", "dp"),
            P(),
            P("dp", "tensor"),
            P("dp", "tensor"),
            P("tensor", "dp"),
        ),
        check_vma=False,
    )
```

time: 146 us -> 126 us (0.86)
  Pallas kernels: 127 us -> 109 us
  local copies, waits for them, and re-layouts: 14.4 us -> 12.4 us
    pallas_call x1, Pallas kernels: 127 us -> 109 us  [block(): pl.pallas_call(kernel, out_shape=[jax.ShapeDtypeStruct((TOK, HALF), BF),...]
    unnamed x28, local copies, waits for them, and re-layouts: 4.77 us -> 2.83 us
where the time goes in v2:
time: 126 us; the launch traced here: 124 us
  Pallas kernels  109 us (87%)
  local copies, waits for them, and re-layouts  12.4 us (10%)
  other arithmetic  2.69 us (2%)
    pallas_call x1, Pallas kernels, block(): pl.pallas_call(kernel, out_shape=[jax.ShapeDtypeStruct((TOK, HALF), BF),...  109 us
    unnamed x28, local copies, waits for them, and re-layouts  2.83 us

profile of v2, /device:TPU:0, one launch (start us, length us, event | category | flops | bytes accessed | tf_op | source)
XLA Modules:
  0.0 124.4 jit_solution(16561845305908265101)
XLA Ops:
  0.7 0.7 add_convert_fusion
  1.4 0.6 broadcast_in_dim.15.code_ref
  2.1 0.7 maximum_convert_fusion.vec_ref
  2.9 0.6 pad_maximum_fusion.pack0
  3.6 0.2 copy-done.6
  3.8 0.1 reshape.60
  3.9 0.7 copy-done.7
  4.7 0.1 reshape.61
  4.9 0.7 fusion.2.pack1
  5.5 0.2 copy-done.8
  5.7 0.1 reshape.62
  5.9 0.6 pad.12.pack2
  6.5 108.5 %shard_map.195 = (bf16[128,512]{1,0:T(8,128)(2,1)}, f32[128,512]{1,0:T(8,128)}, f32[8,1024]{1,0:T(8,128)}, f32[4,16,512]{2,1,0:T(8,128)}, f32[4,16,1280]{2,1,0:T(8,128)}, /*index=5*/f32[4,16,640]{2,1,0:T(8,128)}) custom-call(bf16[128,512]{1,0:T(8,128)(2,1)} %tok_ref.1, bf16[128,512]{1,0:T(8,128)(2,1)} %dy_ref.1, f32[8,128]{1,0:T(8,128)} %broadcast_in_dim.15.code_ref, ...), custom_call_target="tpu_custom_call" | custom-call | tf_op jit(solution)/shard_map/pallas_call | solution.py:831
  115.1 1.4 %fusion.3 = (f32[1,1024]{1,0:T(1,128)}, f32[1,1024]{1,0:T(1,128)}) fusion(f32[8,1024]{1,0:T(8,128)} %get-tuple-element.18), kind=kLoop, calls=%fused_computation.18 | loop fusion | bytes 16384 | tf_op jit(solution)/shard_map/slice | solution.py:882
  116.5 1.4 %slice.26 = f32[3,1024]{1,0:T(4,128)} slice(f32[8,1024]{1,0:T(8,128)} %get-tuple-element.18), slice={[2:5], [0:1024]} | slice | bytes 24576 | tf_op jit(solution)/shard_map/slice | solution.py:882
  117.9 1.4 %copy_bitcast_fusion.4 = f32[512,16]{0,1:T(8,128)} fusion(f32[4,16,512]{2,1,0:T(8,128)} %get-tuple-element.19), kind=kLoop, calls=%fused_computation.13 | loop fusion | bytes 65536 | tf_op jit(solution)/shard_map/reshape | solution.py:878
  119.4 0.7 reshape.64
  120.1 0.2 copy-done.3
  120.4 0.8 reshape.68
  121.2 0.1 copy-done.1
  121.3 0.8 reshape.67
  122.2 0.8 reshape.66
  123.1 0.7 copy.55
  123.7 0.7 copy.56
  (39 shorter events, 0.7 us)
Async XLA Ops:
  0.6 1.4 %copy-start = (bf16[512,16]{0,1:T(8,128)(2,1)S(1)}, bf16[512,16]{0,1:T(8,128)(2,1)}, u32[]{:S(2)}) copy-start(bf16[512,16]{0,1:T(8,128)(2,1)} %param.18) | copy-start | bytes 49156
  1.3 0.7 copy-start.11
  1.3 0.7 copy-start.12
  1.4 0.7 copy-start.10
  1.4 1.3 %copy-start.9 = (bf16[3,16,512]{2,1,0:T(8,128)(2,1)S(1)}, bf16[3,16,512]{2,1,0:T(8,128)(2,1)}, u32[]{:S(2)}) copy-start(bf16[3,16,512]{2,1,0:T(8,128)(2,1)} %param.16) | copy-start | bytes 147460
  2.9 0.9 copy-start.6
  3.8 0.9 copy-start.7
  4.9 0.9 copy-start.8
  115.1 4.2 %copy-start.4 = (f32[4,16,512]{2,1,0:T(8,128)S(1)}, f32[4,16,512]{2,1,0:T(8,128)}, u32[]{:S(2)}) copy-start(f32[4,16,512]{2,1,0:T(8,128)} %get-tuple-element.19) | copy-start | bytes 393220
  119.3 0.9 copy-start.3
  120.3 1.0 copy-start.1
  122.2 0.9 copy-start.5
  122.2 1.5 %copy-start.2 = (f32[128,512]{1,0:T(8,128)S(1)}, f32[128,512]{1,0:T(8,128)}, u32[]{:S(2)}) copy-start(f32[128,512]{1,0:T(8,128)} %get-tuple-element.39) | copy-start | bytes 786436

commit v3 on v2

--- a/solution.py
+++ b/solution.py
@@ -49,10 +49,24 @@
     def __init__(self, copy, time, end):
         self.copy, self.time, self.end, self.waited = copy, time, end, False
 
+    def arrived(self):
+        self.copy.wait_recv()
+
 
 class Group(Event):
     def __init__(self, total):
         self.total, self.sem, self.time, self.waited = total, None, 0.0, False
+
+    def arrived(self):
+        send_sem, recv_sem, device = self.remake
+        pltpu.make_async_remote_copy(
+            src_ref=self.total,
+            dst_ref=self.total,
+            send_sem=send_sem,
+            recv_sem=recv_sem,
+            device_id=device,
+            device_id_type=pl.DeviceIdType.MESH,
+        ).wait_recv()
 
 
 class Room:
@@ -109,14 +123,7 @@
         if group is None:
             return self.pool[k]
         group.sem, group.time = sem, max(group.time, end + latency)
-        group.copy = pltpu.make_async_remote_copy(
-            src_ref=group.total,
-            dst_ref=group.total,
-            send_sem=self.send_sems.at[k],
-            recv_sem=self.recv_sems.at[sem],
-            device_id=device,
-            device_id_type=pl.DeviceIdType.MESH,
-        )
+        group.remake = (self.send_sems.at[k], self.recv_sems.at[sem], device)
         return group
 
     def room(self, link, slack=0.8):
@@ -143,7 +150,7 @@
             task = self.tasks[i]
             for event in task[2]:
                 if isinstance(event, (Copy, Group)) and not event.waited:
-                    event.copy.wait_recv()
+                    event.arrived()
                     event.waited = True
                     self.now += 0.03
             try:
@@ -199,20 +206,54 @@
     yield [rest]
 
 
+def low_lanes():
+    return lax.broadcasted_iota(jnp.int32, (16, CH), 1) < CH // 2
+
+
+def half_tile(tile, odd):
+    return jnp.where(low_lanes(), pltpu.roll(tile, CH // 2, 1) if odd else tile, 0.0)
+
+
+def whole_tile(even, odd):
+    return jnp.where(low_lanes(), even.astype(F32), pltpu.roll(odd.astype(F32), CH // 2, 1))
+
+
 def kernel(
-    tok_ref,
-    dy_ref,
-    code_ref,
-    vec_ref,
-    pack0,
-    pack1,
-    pack2,
+    tok_hbm,
+    dy_hbm,
+    seg_hbm,
+    valid_hbm,
+    gain1_hbm,
+    gain2_hbm,
+    conv_hbm,
+    in_hbm,
+    out_hbm,
+    gate_hbm,
+    up_hbm,
+    down_hbm,
     mix_out,
     tg_out,
     small_out,
     g0_out,
     g1_out,
     g2_out,
+    tok_ref,
+    dy_ref,
+    vec_ref,
+    seg_ref,
+    valid_ref,
+    gain1_ref,
+    gain2_ref,
+    conv_ref,
+    in_ref,
+    out_ref,
+    gate_ref,
+    up_ref,
+    down_ref,
+    code_ref,
+    pack0,
+    pack1,
+    pack2,
     w0,
     w1,
     w2,
@@ -265,6 +306,7 @@
     uu,
     dab,
     red,
+    load_sems,
     send_sems,
     recv_sems,
 ):
@@ -290,6 +332,41 @@
     others = [peer, after, before] + xs[1:] + ys[1:] + zs[1:]
     for other in others:
         pl.semaphore_signal(barrier, inc=1, device_id=other, device_id_type=pl.DeviceIdType.MESH)
+    loads = [
+        pltpu.make_async_copy(src, dst, load_sems.at[k])
+        for k, (src, dst) in enumerate(
+            (
+                (seg_hbm, seg_ref),
+                (valid_hbm, valid_ref),
+                (gain1_hbm, gain1_ref),
+                (gain2_hbm, gain2_ref),
+                (conv_hbm, conv_ref),
+                (in_hbm, in_ref),
+                (out_hbm, out_ref),
+                (tok_hbm, tok_ref),
+                (gate_hbm, gate_ref),
+                (up_hbm, up_ref),
+                (down_hbm, down_ref),
+                (dy_hbm, dy_ref),
+            )
+        )
+    ]
+    for load in loads:
+        load.start()
+    for load in loads:
+        load.wait()
+    vec_ref[0] = gain1_ref[...].astype(F32)
+    vec_ref[1] = gain2_ref[...].astype(F32)
+    vec_ref[2:5] = conv_ref[...].astype(F32)
+    code_ref[...] = jnp.broadcast_to((seg_ref[...] + 16 * valid_ref[...]).astype(F32)[None], (8, CH))
+    for j in range(R):
+        for k in range(3):
+            pack0[j, :, k * CH : (k + 1) * CH] = in_ref[k, :, j * CH : (j + 1) * CH]
+        pack0[j, :, 3 * CH :] = out_ref[:, j * CH : (j + 1) * CH]
+        cols, tile = slice(j * HALF, (j + 1) * HALF), slice(2048 + j // 2 * CH, 2048 + (j // 2 + 1) * CH)
+        for pack, k, ref in ((pack1, 0, gate_ref), (pack1, HP, up_ref), (pack2, 0, down_ref)):
+            pack[j, :, k : k + HALF] = ref[:, cols]
+            pack[j, :, k + HALF : k + HP] = half_tile(ref[:, tile].astype(F32), j % 2).astype(BF)
     pl.semaphore_wait(barrier, len(others))
 
     s = Schedule(send_sems, recv_sems)
@@ -755,7 +832,7 @@
             s.send(rows(up(z, k)), oas[c].at[z, :, ln], zs[k], *z_links[k], group=group)
         oas[c][z, :, ln] = rows(z)[...]
         yield [group]
-        outs[c][:, :, ln] = oas[c][:, :, ln].astype(F32)
+        outs[c][:, :, ln] = oas[c][:, :, ln]
         s.work(0.2)
 
     s.add(0, halo())
@@ -779,11 +856,49 @@
     s.run()
 
 
-def block(tokens, dy, code, vec, pack0, pack1, pack2):
+def finish(mix, tg, small, p0, p1, p2, o_mix, o_tg, o_gain1, o_in, o_conv, o_out, o_gain2, o_gate, o_up, o_down):
+    o_mix[...] = mix[...]
+    o_tg[...] = tg[...]
+    o_gain1[...] = small[0]
+    o_gain2[...] = small[1]
+    o_conv[...] = small[2:5]
+    for j in range(R):
+        for k in range(3):
+            o_in[k, :, j * CH : (j + 1) * CH] = p0[j, :, k * CH : (k + 1) * CH].astype(F32)
+        o_out[:, j * CH : (j + 1) * CH] = p0[j, :, 3 * CH :].astype(F32)
+        cols = slice(j * HALF, (j + 1) * HALF)
+        o_gate[:, cols] = p1[j, :, 0:HALF].astype(F32)
+        o_up[:, cols] = p1[j, :, HP : HP + HALF].astype(F32)
+        o_down[:, cols] = p2[j, :, 0:HALF].astype(F32)
+    for t in range(2):
+        tile = slice(2048 + t * CH, 2048 + (t + 1) * CH)
+        o_gate[:, tile] = whole_tile(p1[2 * t, :, HALF:HP], p1[2 * t + 1, :, HALF:HP])
+        o_up[:, tile] = whole_tile(p1[2 * t, :, HP + HALF :], p1[2 * t + 1, :, HP + HALF :])
+        o_down[:, tile] = whole_tile(p2[2 * t, :, HALF:HP], p2[2 * t + 1, :, HALF:HP])
+
+
+def block(tokens, dy, seg, valid, gain1, gain2, conv, in_weight, out_weight, gate, up, down):
     vmem = pl.BlockSpec(memory_space=pltpu.VMEM)
+    loaded = [
+        pltpu.VMEM((TOK, HALF), BF),
+        pltpu.VMEM((TOK, HALF), BF),
+        pltpu.VMEM((8, D), F32),
+        pltpu.VMEM((TOK,), jnp.int32),
+        pltpu.VMEM((TOK,), jnp.int32),
+        pltpu.VMEM((D,), BF),
+        pltpu.VMEM((D,), BF),
+        pltpu.VMEM((3, D), BF),
+        pltpu.VMEM((3, 16, HALF), BF),
+        pltpu.VMEM((16, HALF), BF),
+        pltpu.VMEM((16, R * HID), BF),
+        pltpu.VMEM((16, R * HID), BF),
+        pltpu.VMEM((16, R * HID), BF),
+        pltpu.VMEM((8, CH), F32),
+    ] + [pltpu.VMEM((R, 16, w), BF) for w in WIDTHS]
     plane = [pltpu.VMEM((4, 4, 64, w), BF) for w in WIDTHS]
     scratch = (
-        plane
+        loaded
+        + plane
         + [pltpu.VMEM((4, 4, 64, w), BF) for w in WIDTHS]
         + [pltpu.VMEM((2, 6, 4, 16, w), BF) for w in (512, HP, HP, HP)]
         + [pltpu.VMEM((2, 6, 16, w), BF) for w in (512, HP, HP, HP)]
@@ -824,25 +939,43 @@
             pltpu.VMEM((GT, HP), BF),
             pltpu.VMEM((GT, 2 * HP), BF),
             pltpu.VMEM((4, 4, 8, D), F32),
+            pltpu.SemaphoreType.DMA((12,)),
             pltpu.SemaphoreType.DMA((SENDS,)),
             pltpu.SemaphoreType.DMA((RECEIVES,)),
         ]
     )
-    return pl.pallas_call(
+    packed = pl.pallas_call(
         kernel,
         out_shape=[
             jax.ShapeDtypeStruct((TOK, HALF), BF),
             jax.ShapeDtypeStruct((TOK, HALF), F32),
             jax.ShapeDtypeStruct((8, D), F32),
         ]
-        + [jax.ShapeDtypeStruct((4, 16, w), F32) for w in WIDTHS],
-        in_specs=[vmem] * 7,
+        + [jax.ShapeDtypeStruct((R, 16, w), BF) for w in WIDTHS],
+        in_specs=[pl.BlockSpec(memory_space=pl.ANY)] * 12,
         out_specs=[vmem] * 6,
         scratch_shapes=scratch,
         compiler_params=pltpu.CompilerParams(
             collective_id=0, has_side_effects=True, vmem_limit_bytes=58 * 1024 * 1024
         ),
-    )(tokens, dy, code, vec, pack0, pack1, pack2)
+    )(tokens, dy, seg, valid, gain1, gain2, conv, in_weight, out_weight, gate, up, down)
+    return pl.pallas_call(
+        finish,
+        out_shape=[
+            jax.ShapeDtypeStruct((TOK, HALF), BF),
+            jax.ShapeDtypeStruct((TOK, HALF), F32),
+            jax.ShapeDtypeStruct((D,), F32),
+            jax.ShapeDtypeStruct((3, 16, HALF), F32),
+            jax.ShapeDtypeStruct((3, D), F32),
+            jax.ShapeDtypeStruct((16, HALF), F32),
+            jax.ShapeDtypeStruct((D,), F32),
+            jax.ShapeDtypeStruct((16, R * HID), F32),
+            jax.ShapeDtypeStruct((16, R * HID), F32),
+            jax.ShapeDtypeStruct((16, R * HID), F32),
+        ],
+        in_specs=[vmem] * 6,
+        out_specs=[vmem] * 10,
+    )(*packed)
 
 
 def local(
@@ -859,27 +992,24 @@
     down_weight,
     out_cotangent,
 ):
-    code = (segment_ids + 16 * valid_mask).astype(F32)
-    code = jnp.broadcast_to(code[None], (8, CH))
-    vec = jnp.concatenate(
-        [norm1_gain[None], norm2_gain[None], conv_weight, jnp.zeros((3, D), BF)], axis=0
-    ).astype(F32)
-
-    def wide(w):
-        return jnp.pad(w.reshape(16, 4, HID).transpose(1, 0, 2), ((0, 0), (0, 0), (0, HP - HID)))
-
-    ins = in_weight.reshape(3, 16, 4, CH).transpose(2, 1, 0, 3).reshape(4, 16, 3 * CH)
-    outs = out_weight.reshape(4, CH, 16).transpose(0, 2, 1)
-    pack0 = jnp.concatenate([ins, outs], axis=2)
-    pack1 = jnp.concatenate([wide(gate_weight), wide(up_weight)], axis=2)
-    pack2 = jnp.pad(down_weight.reshape(4, HID, 16).transpose(0, 2, 1), ((0, 0), (0, 0), (0, HP - HID)))
-    mixed, tokens_grad, small, p0, p1, p2 = block(tokens, out_cotangent, code, vec, pack0, pack1, pack2)
-    grad_in = p0[:, :, : 3 * CH].reshape(4, 16, 3, CH).transpose(2, 1, 0, 3).reshape(3, 16, HALF)
-    grad_out = p0[:, :, 3 * CH :].transpose(0, 2, 1).reshape(HALF, 16)
-    grad_gate = p1[:, :, :HID].transpose(1, 0, 2).reshape(16, 4 * HID)
-    grad_up = p1[:, :, HP : HP + HID].transpose(1, 0, 2).reshape(16, 4 * HID)
-    grad_down = p2[:, :, :HID].transpose(0, 2, 1).reshape(4 * HID, 16)
-    return (mixed, tokens_grad, small[0], grad_in, small[2:5], grad_out, small[1], grad_gate, grad_up, grad_down)
+    outs = list(
+        block(
+            tokens,
+            out_cotangent,
+            segment_ids,
+            valid_mask,
+            norm1_gain,
+            norm2_gain,
+            conv_weight,
+            in_weight,
+            out_weight.T,
+            gate_weight,
+            up_weight,
+            down_weight.T,
+        )
+    )
+    outs[5], outs[9] = outs[5].T, outs[9].T
+    return tuple(outs)
 
 
 def solution(mesh):

time: 126 us -> 112 us (0.89)
  local copies, waits for them, and re-layouts: 12.4 us -> 0 us
  other arithmetic: 2.69 us -> 0 us
    reshape x13 -> x0, local copies, waits for them, and re-layouts: 5.07 us -> none  [the longest x1 1.37 us: local(): grad_out = p0[:, :, 3 * CH:].transpose(0, 2, 1).reshape(HALF, 16)]
    unnamed x28 -> x0, local copies, waits for them, and re-layouts: 2.83 us -> none
    slice x3 -> x0, local copies, waits for them, and re-layouts: 2.81 us -> none  [the longest x1 1.44 us: local(): small[1]]
    pallas_call x0 -> x1, Pallas kernels: none -> 2.13 us  [block(): pl.pallas_call(finish, out_shape=[jax.ShapeDtypeStruct((TOK, HALF), BF),...]
    convert_element_type x2 -> x0, other arithmetic: 1.37 us -> none  [the longest x1 0.69 us: local(): vec = jnp.concatenate([norm1_gain[None], norm2_gain[None], conv_weight, j...]
    concatenate x2 -> x0, other arithmetic: 1.32 us -> none  [the longest x1 0.68 us: local(): pack1 = jnp.concatenate([wide(gate_weight), wide(up_weight)], axis=2)]
where the time goes in v3:
time: 112 us; the launch traced here: 110 us
  Pallas kernels  110 us (98%)
    pallas_call x1, Pallas kernels, block(): pl.pallas_call(kernel, out_shape=[jax.ShapeDtypeStruct((TOK, HALF), BF),...  108 us

profile of v3, /device:TPU:0, one launch (start us, length us, event | category | flops | bytes accessed | tf_op | source)
XLA Modules:
  0.0 110.5 jit_solution(18374161209881991066)
XLA Ops:
  0.6 107.7 %shard_map.195 = (bf16[128,512]{1,0:T(8,128)(2,1)}, f32[128,512]{1,0:T(8,128)}, f32[8,1024]{1,0:T(8,128)}, bf16[4,16,512]{2,1,0:T(8,128)(2,1)}, bf16[4,16,1280]{...) custom-call(bf16[128,512]{1,0:T(8,128)(2,1)} %tok_hbm.1, bf16[128,512]{1,0:T(8,128)(2,1)} %dy_hbm.1, s32[128]{0:T(128)} %seg_hbm.1, ...), custom_call_target="tpu_custom_call" | custom-call | tf_op jit(solution)/shard_map/pallas_call | solution.py:947
  108.4 2.1 %shard_map.196 = (bf16[128,512]{1,0:T(8,128)(2,1)}, f32[128,512]{1,0:T(8,128)}, f32[1024]{0:T(1024)}, f32[3,16,512]{2,1,0:T(8,128)}, f32[3,1024]{1,0:T(4,128)}, ...) custom-call(bf16[128,512]{1,0:T(8,128)(2,1)} %get-tuple-element.26.mix, ...), custom_call_target="tpu_custom_call" | custom-call | tf_op jit(solution)/shard_map/pallas_call | solution.py:962

commit v4 on v3

--- a/solution.py
+++ b/solution.py
@@ -17,8 +17,9 @@
 HID = 576
 HP = 640
 WIDTHS = (512, 2 * HP, HP)
+BVC = (0, 2, 1)
 SENDS = 48
-RECEIVES = 186
+RECEIVES = 200
 
 
 def nn(a, b):
@@ -75,21 +76,23 @@
 
     @property
     def time(self):
+        if self.link in self.schedule.quiet:
+            return float("inf")
         return self.schedule.free.get(self.link, 0.0) - self.slack
 
 
 class Schedule:
-    RATE = 46.8e3
+    RATE = 38.0e3
     CORE_RATE = 700e3
-    LATENCY = 1.65
-    FAR_LATENCY = 2.3
-    CORE_LATENCY = 0.9
+    LATENCY = 2.6
+    FAR_LATENCY = 3.6
+    CORE_LATENCY = 1.7
     ISSUE = 0.05
 
     def __init__(self, send_sems, recv_sems):
         self.send_sems, self.recv_sems = send_sems, recv_sems
-        self.pool, self.received = [None] * SENDS, 0
-        self.tasks, self.free, self.now = [], {}, 2.0
+        self.pool, self.received, self.quiet = [None] * SENDS, 0, ()
+        self.tasks, self.free, self.now = [], {}, 3.7
 
     def send(self, src, dst, device, *links, group=None):
         k = min(range(SENDS), key=lambda i: -1.0 if self.pool[i] is None else self.pool[i].end)
@@ -126,7 +129,7 @@
         group.remake = (self.send_sems.at[k], self.recv_sems.at[sem], device)
         return group
 
-    def room(self, link, slack=0.8):
+    def room(self, link, slack=12.0):
         return [Room(self, link, slack)]
 
     def work(self, us):
@@ -233,7 +236,7 @@
     down_hbm,
     mix_out,
     tg_out,
-    small_out,
+    small_sum,
     g0_out,
     g1_out,
     g2_out,
@@ -264,10 +267,12 @@
     ra1,
     ra2,
     ra3,
+    ra4,
     rb0,
     rb1,
     rb2,
     rb3,
+    rb4,
     oa0,
     oa1,
     oa2,
@@ -306,6 +311,8 @@
     uu,
     dab,
     red,
+    redc,
+    small_out,
     load_sems,
     send_sems,
     recv_sems,
@@ -361,7 +368,7 @@
     code_ref[...] = jnp.broadcast_to((seg_ref[...] + 16 * valid_ref[...]).astype(F32)[None], (8, CH))
     for j in range(R):
         for k in range(3):
-            pack0[j, :, k * CH : (k + 1) * CH] = in_ref[k, :, j * CH : (j + 1) * CH]
+            pack0[j, :, k * CH : (k + 1) * CH] = in_ref[BVC[k], :, j * CH : (j + 1) * CH]
         pack0[j, :, 3 * CH :] = out_ref[:, j * CH : (j + 1) * CH]
         cols, tile = slice(j * HALF, (j + 1) * HALF), slice(2048 + j // 2 * CH, 2048 + (j // 2 + 1) * CH)
         for pack, k, ref in ((pack1, 0, gate_ref), (pack1, HP, up_ref), (pack2, 0, down_ref)):
@@ -370,10 +377,11 @@
     pl.semaphore_wait(barrier, len(others))
 
     s = Schedule(send_sems, recv_sems)
-    packs, ws, gs = (pack0, pack1, pack1, pack2), (w0, w1, w1, w2), (g0, g1, g1, g2)
-    ras, rbs, oas = (ra0, ra1, ra2, ra3), (rb0, rb1, rb2, rb3), (oa0, oa1, oa1, oa2)
-    outs = (g0_out, g1_out, g1_out, g2_out)
+    packs, ws, gs = (pack0, pack1, pack1, pack2), (w0, w1, w1, w2), (g0, g1, g1, g2, g0)
+    ras, rbs, oas = (ra0, ra1, ra2, ra3, ra4), (rb0, rb1, rb2, rb3, rb4), (oa0, oa1, oa1, oa2, oa0)
+    outs = (g0_out, g1_out, g1_out, g2_out, g0_out)
     lanes = (pl.ds(0, 512), pl.ds(0, HP), pl.ds(HP, HP), pl.ds(0, HP))
+    grad_lanes = (pl.ds(2 * CH, 2 * CH),) + lanes[1:] + (pl.ds(0, 2 * CH),)
     my_cols = pl.ds(pl.multiple_of(core * HALF, HALF), HALF)
     peer_cols = pl.ds(pl.multiple_of((1 - core) * HALF, HALF), HALF)
     ch_cols = pl.ds(pl.multiple_of(core * HALF + z * CH, CH), CH)
@@ -404,7 +412,7 @@
         return side_a, side_b
 
     def rs_plane(c):
-        g, ra, rb, ln, us = gs[c], ras[c], rbs[c], lanes[c], 0.12
+        g, ra, rb, ln, us = gs[c], ras[c], rbs[c], grad_lanes[c], 0.12
 
         def part(base, h):
             return pl.ds(base + 16 * h, 16)
@@ -470,6 +478,8 @@
         core_too(1, prev, 1)
         yield [c4]
         core_too(2, nxt, 0)
+        if n is dhb:
+            s.quiet = ("x-", "y-")
         yield [to_core[1]]
         s.done(have[1])
         yield [to_core[2]]
@@ -551,7 +561,7 @@
     dealt, full_w, issued = events(4), events(4, 2), events(4, 2)
     have_n1, have_n2, have_dy, have_dh = events(4), events(4), events(4), events(4)
     sent_n1, sent_n2, sent_dy, sent_dh = events(4)
-    have_codes, have_halo, ffn, conv_back, sums = events(5)
+    have_codes, have_halo, ffn, c_back, conv_back, sums = events(6)
     gain1 = vec_ref[pl.ds(0, 1), my_cols]
     gain2 = vec_ref[pl.ds(1, 1), my_cols]
     taps = [vec_ref[pl.ds(2 + k, 1), ch_cols] for k in range(3)]
@@ -585,8 +595,8 @@
 
     def halo():
         yield [
-            s.send(tok_ref.at[pl.ds(TOK - 16, 16)], tail_raw, after, "x+"),
-            s.send(code_ref, tail_code.at[z], after, "x+"),
+            s.send(tok_ref.at[pl.ds(TOK - 16, 16)], tail_raw, after, "x+", "y+"),
+            s.send(code_ref, tail_code.at[z], after, "x+", "y+"),
         ]
         tok = tail_raw[...].astype(F32)
         tail_s[...] = jnp.broadcast_to(jnp.sum(tok * tok, axis=1, keepdims=True), (16, CH))
@@ -643,7 +653,7 @@
         du = nn(dyf[rows, :], w2[...].reshape(D, HP))
         dab[rows, 0:HP] = (du * b * sg * (1.0 + a * (1.0 - sg))).astype(BF)
         dab[rows, HP : 2 * HP] = (du * silu).astype(BF)
-        s.work(1.0)
+        s.work(0.9)
 
     def y_part(j):
         rows = rows_of(j)
@@ -652,8 +662,10 @@
 
     def n2_part(j):
         rows = rows_of(j)
-        zpart[1, rows, :] = nt(dab[rows, :], w1[...].reshape(D, 2 * HP)).astype(BF)
-        s.work(0.6)
+        part = nt(dab[rows, :], w1[...].reshape(D, 2 * HP))
+        zpart[1, rows, :] = part.astype(BF)
+        small_out[pl.ds(1, 1), :] += jnp.sum(part * n2[rows, :].astype(F32), axis=0, keepdims=True)
+        s.work(0.9)
 
     def u_part(j):
         rows = rows_of(j)
@@ -662,13 +674,17 @@
 
     def n1_part(j):
         rows = rows_of(j)
-        zpart[3, rows, :] = nt(dbcv[rows, :], w0[...].reshape(D, 512)[:, : 3 * CH]).astype(BF)
-        s.work(0.25)
+        part = nt(dbcv[rows, :], w0[...].reshape(D, 512)[:, : 3 * CH])
+        zpart[3, rows, :] = part.astype(BF)
+        small_out[pl.ds(0, 1), :] += jnp.sum(part * n1[rows, :].astype(F32), axis=0, keepdims=True)
+        s.work(0.35)
+        if j is z:
+            s.done(sums)
 
     def main():
         yield have_n1 + full_w[0] + [have_halo]
         bcv[...] = nn(n1[...], w0[...].reshape(D, 512)[:, : 3 * CH])
-        mixed = (bcv[:, 0:CH] * bcv[:, 2 * CH : 3 * CH]).astype(BF).astype(F32)
+        mixed = (bcv[:, 0:CH] * bcv[:, CH : 2 * CH]).astype(BF).astype(F32)
         mx[pl.ds(8, GT), :] = mixed[:GT]
         mx[pl.ds(0, 8), :] = mixed[GT + 8 :]
         s.work(1.0)
@@ -678,7 +694,7 @@
             + taps[1] * mx[pl.ds(7, GT), :] * keep(1)
             + taps[2] * mx[pl.ds(6, GT), :] * keep(2)
         )
-        gat[...] = (bcv[pl.ds(0, GT), CH : 2 * CH] * zc[...]).astype(BF)
+        gat[...] = (bcv[pl.ds(0, GT), 2 * CH : 3 * CH] * zc[...]).astype(BF)
         s.work(0.4)
         yield from rs_group(0, y_part)
         h2s[...] = tok_ref[...].astype(F32) + rs_result(0)
@@ -693,6 +709,7 @@
         s.add(1, ag_group(n2, have_n2, sent_n2))
         yield have_dy + full_w[1] + full_w[2] + full_w[3]
         last = Group(zd)
+        small_out[...] = jnp.zeros((8, D), F32)
         for j, event, copy in ((z, have_n2[0], 0), (prev, have_n2[1], 3), (nxt, have_n2[2], 1), (far, have_n2[3], 2)):
             yield [event]
             ffn_block(j)
@@ -706,8 +723,6 @@
         yield block_sent
         yield [last]
         dn2 = rs_result(1)
-        small_out[...] = jnp.zeros((8, D), F32)
-        small_out[pl.ds(1, 1), my_cols] = jnp.sum(dn2 * hat2[...], axis=0, keepdims=True)
         e2 = dn2 * gain2
         copy = chip_sum(2, e2 * hat2[...])
         s.work(0.4)
@@ -721,15 +736,17 @@
         yield from ag_group(dhb, have_dh, sent_dh)
 
         dg = nn(dhb[...], w0[...].reshape(D, 512)[:, 3 * CH :])
-        dbcv[:, CH : 2 * CH] = (dg * zc[...]).astype(BF)
-        dz = dg * bcv[pl.ds(0, GT), CH : 2 * CH]
+        dbcv[:, 2 * CH : 3 * CH] = (dg * zc[...]).astype(BF)
+        dz = dg * bcv[pl.ds(0, GT), 2 * CH : 3 * CH]
         q0[...] = dz * keep(0)
         q1[pl.ds(0, GT), :] = dz * keep(1)
         q2[pl.ds(0, GT), :] = dz * keep(2)
         halo_s[0] = q1[pl.ds(0, 8), :]
         halo_s[1] = q2[pl.ds(0, 8), :]
         s.work(0.6)
-        copy = s.send(halo_s, halo_r, before, "x-")
+        s.quiet = ()
+        copy = s.send(halo_s, halo_r, before, "x-", "y-")
+        s.done(c_back)
         small_out[pl.ds(2, 1), ch_cols] = jnp.sum(q0[...] * mx[pl.ds(8, GT), :], axis=0, keepdims=True)
         small_out[pl.ds(3, 1), ch_cols] = jnp.sum(q1[pl.ds(0, GT), :] * mx[pl.ds(7, GT), :], axis=0, keepdims=True)
         small_out[pl.ds(4, 1), ch_cols] = jnp.sum(q2[pl.ds(0, GT), :] * mx[pl.ds(6, GT), :], axis=0, keepdims=True)
@@ -739,19 +756,17 @@
         q1[pl.ds(GT, 8), :] = jnp.where(last, 0.0, halo_r[0])
         q2[pl.ds(GT, 8), :] = jnp.where(last, 0.0, halo_r[1])
         dm = taps[0] * q0[...] + taps[1] * q1[pl.ds(1, GT), :] + taps[2] * q2[pl.ds(2, GT), :]
-        dbcv[:, 0:CH] = (dm * bcv[pl.ds(0, GT), 2 * CH : 3 * CH]).astype(BF)
-        dbcv[:, 2 * CH : 3 * CH] = (dm * bcv[pl.ds(0, GT), 0:CH]).astype(BF)
+        dbcv[:, 0:CH] = (dm * bcv[pl.ds(0, GT), CH : 2 * CH]).astype(BF)
+        dbcv[:, CH : 2 * CH] = (dm * bcv[pl.ds(0, GT), 0:CH]).astype(BF)
         s.work(0.4)
         s.done(conv_back)
         yield []
 
         yield from rs_group(3, n1_part)
         dn1 = rs_result(3)
-        small_out[pl.ds(0, 1), my_cols] = jnp.sum(dn1 * hat1[...], axis=0, keepdims=True)
         e1 = dn1 * gain1
         copy = chip_sum(3, e1 * hat1[...])
         s.work(0.4)
-        s.done(sums)
         yield [copy]
         m1 = chip_total(3) * (1.0 / D)
         r1 = lax.rsqrt(chip_total(0) * (1.0 / D) + EPS)
@@ -761,17 +776,22 @@
 
     def small_sums():
         yield [sums]
+        yield [s.send(small_out.at[:, peer_cols], redc.at[2], peer, "c")]
+        half = small_out[:, my_cols] + redc[2]
         for k, (axis, i, peers) in enumerate((("x", x, xs), ("y", y, ys), ("z", z, zs))):
-            red[k, i] = small_out[...]
+            red[k, i] = half
             group = Group(red.at[k, pl.ds(0, 3)])
-            for j in (1, 3, 2):
+            for j in (2, 1, 3):
                 s.send(red.at[k, i], red.at[k, i], peers[j], *links[axis][j], group=group)
             yield [group]
-            small_out[...] = (red[k, 0] + red[k, 1]) + (red[k, 2] + red[k, 3])
+            half = (red[k, 0] + red[k, 1]) + (red[k, 2] + red[k, 3])
             s.work(0.1)
-        red[3, core] = small_out[...]
-        yield [s.send(red.at[3, core], red.at[3, core], peer, "c")]
-        small_out[...] = red[3, 0] + red[3, 1]
+        redc[core] = half
+        yield [s.send(redc.at[core], redc.at[core], peer, "c")]
+        for h in range(2):
+            cols = pl.ds(h * HALF, HALF)
+            small_sum[0:2, cols] = redc[h, 0:2] / vec_ref[0:2, cols]
+            small_sum[2:8, cols] = redc[h, 2:8]
 
     block_sent = events(4)
 
@@ -792,7 +812,7 @@
         def step(i):
             ln = lanes[1 + h]
             g1[i, :, :, ln] = tn(n2[:, pl.ds(i * 256, 256)], dab[:, ln]).astype(BF).reshape(4, 64, HP)
-            s.work(0.4)
+            s.work(0.3)
 
         return step
 
@@ -802,11 +822,16 @@
 
     def make_g0(i):
         cols = pl.ds(i * 256, 256)
-        g0[i, :, :, 0 : 3 * CH] = tn(n1[pl.ds(0, GT), cols], dbcv[...]).astype(BF).reshape(4, 64, 3 * CH)
-        g0[i, :, :, 3 * CH : 4 * CH] = tn(dhb[:, cols], gat[...]).astype(BF).reshape(4, 64, CH)
-        s.work(0.35)
-
-    made, summed = events(4), events(4, 2)
+        g0[i, :, :, 2 * CH : 3 * CH] = tn(n1[pl.ds(0, GT), cols], dbcv[:, 2 * CH :]).astype(BF).reshape(4, 64, CH)
+        g0[i, :, :, 3 * CH :] = tn(dhb[:, cols], gat[...]).astype(BF).reshape(4, 64, CH)
+        s.work(0.2)
+
+    def make_g4(i):
+        cols = pl.ds(i * 256, 256)
+        g0[i, :, :, 0 : 2 * CH] = tn(n1[pl.ds(0, GT), cols], dbcv[:, 0 : 2 * CH]).astype(BF).reshape(4, 64, 2 * CH)
+        s.work(0.2)
+
+    made, summed = events(5), events(5, 2)
 
     def make(c, after_event, step):
         yield [after_event]
@@ -822,7 +847,7 @@
 
     def hand_back(c):
         yield summed[c]
-        ln = lanes[c]
+        ln = grad_lanes[c]
 
         def rows(j):
             return gs[c].at[y, x, pl.ds(pl.multiple_of(j * 16, 16), 16), ln]
@@ -846,11 +871,17 @@
         for h, side in enumerate(ag_plane(c, issued)):
             s.add(2 + c, gather_side(c, h, side))
     s.add(7, main())
-    for c, after_event, step in ((1, ffn, make_half(0)), (2, ffn, make_half(1)), (3, ffn, make_g2), (0, conv_back, make_g0)):
-        s.add(8 + c, make(c, after_event, step))
+    for c, rank, after_event, step in (
+        (1, 3, ffn, make_half(0)),
+        (2, 4, ffn, make_half(1)),
+        (3, 5, ffn, make_g2),
+        (0, 2, c_back, make_g0),
+        (4, 1, conv_back, make_g4),
+    ):
+        s.add(7 + rank, make(c, after_event, step))
         for h, side in enumerate(rs_plane(c)):
-            s.add(2 + c, reduce_side(c, h, side))
-        s.add(4, hand_back(c))
+            s.add(rank, reduce_side(c, h, side))
+        s.add(rank, hand_back(c))
     s.add(13, hidden_out())
     s.add(2, small_sums())
     s.run()
@@ -864,7 +895,7 @@
     o_conv[...] = small[2:5]
     for j in range(R):
         for k in range(3):
-            o_in[k, :, j * CH : (j + 1) * CH] = p0[j, :, k * CH : (k + 1) * CH].astype(F32)
+            o_in[BVC[k], :, j * CH : (j + 1) * CH] = p0[j, :, k * CH : (k + 1) * CH].astype(F32)
         o_out[:, j * CH : (j + 1) * CH] = p0[j, :, 3 * CH :].astype(F32)
         cols = slice(j * HALF, (j + 1) * HALF)
         o_gate[:, cols] = p1[j, :, 0:HALF].astype(F32)
@@ -900,8 +931,8 @@
         loaded
         + plane
         + [pltpu.VMEM((4, 4, 64, w), BF) for w in WIDTHS]
-        + [pltpu.VMEM((2, 6, 4, 16, w), BF) for w in (512, HP, HP, HP)]
-        + [pltpu.VMEM((2, 6, 16, w), BF) for w in (512, HP, HP, HP)]
+        + [pltpu.VMEM((2, 6, 4, 16, w), BF) for w in (2 * CH, HP, HP, HP, 2 * CH)]
+        + [pltpu.VMEM((2, 6, 16, w), BF) for w in (2 * CH, HP, HP, HP, 2 * CH)]
         + [pltpu.VMEM((4, 16, w), BF) for w in WIDTHS]
         + [
             pltpu.VMEM((4, 8, CH), F32),
@@ -938,7 +969,9 @@
             pltpu.VMEM((2, 8, CH), F32),
             pltpu.VMEM((GT, HP), BF),
             pltpu.VMEM((GT, 2 * HP), BF),
-            pltpu.VMEM((4, 4, 8, D), F32),
+            pltpu.VMEM((3, R, 8, HALF), F32),
+            pltpu.VMEM((3, 8, HALF), F32),
+            pltpu.VMEM((8, D), F32),
             pltpu.SemaphoreType.DMA((12,)),
             pltpu.SemaphoreType.DMA((SENDS,)),
             pltpu.SemaphoreType.DMA((RECEIVES,)),

time: 112 us -> 104 us (0.929)
  Pallas kernels: 110 us -> 103 us
    pallas_call x1, Pallas kernels: 108 us -> 101 us  [block(): pl.pallas_call(kernel, out_shape=[jax.ShapeDtypeStruct((TOK, HALF), BF),...]
where the time goes in v4:
time: 104 us; the launch traced here: 103 us
  Pallas kernels  103 us (99%)
    pallas_call x1, Pallas kernels, block(): pl.pallas_call(kernel, out_shape=[jax.ShapeDtypeStruct((TOK, HALF), BF),...  101 us
    pallas_call x1, Pallas kernels, block(): pl.pallas_call(finish, out_shape=[jax.ShapeDtypeStruct((TOK, HALF), BF),...  2.13 us

profile of v4, /device:TPU:0, one launch (start us, length us, event | category | flops | bytes accessed | tf_op | source)
XLA Modules:
  0.0 103.5 jit_solution(6002882657482956573)
XLA Ops:
  0.6 100.7 %shard_map.195 = (bf16[128,512]{1,0:T(8,128)(2,1)}, f32[128,512]{1,0:T(8,128)}, f32[8,1024]{1,0:T(8,128)}, bf16[4,16,512]{2,1,0:T(8,128)(2,1)}, bf16[4,16,1280]{...) custom-call(bf16[128,512]{1,0:T(8,128)(2,1)} %tok_hbm.1, bf16[128,512]{1,0:T(8,128)(2,1)} %dy_hbm.1, s32[128]{0:T(128)} %seg_hbm.1, ...), custom_call_target="tpu_custom_call" | custom-call | tf_op jit(solution)/shard_map/pallas_call | solution.py:980
  101.4 2.1 %shard_map.196 = (bf16[128,512]{1,0:T(8,128)(2,1)}, f32[128,512]{1,0:T(8,128)}, f32[1024]{0:T(1024)}, f32[3,16,512]{2,1,0:T(8,128)}, f32[3,1024]{1,0:T(4,128)}, ...) custom-call(bf16[128,512]{1,0:T(8,128)(2,1)} %get-tuple-element.26.mix, ...), custom_call_target="tpu_custom_call" | custom-call | tf_op jit(solution)/shard_map/pallas_call | solution.py:995

commit v5 on v4

--- a/solution.py
+++ b/solution.py
@@ -16,7 +16,8 @@
 CH = 128
 HID = 576
 HP = 640
-WIDTHS = (512, 2 * HP, HP)
+GW = 1152
+WIDTHS = (512, GW, HP)
 BVC = (0, 2, 1)
 SENDS = 48
 RECEIVES = 200
@@ -82,7 +83,7 @@
 
 
 class Schedule:
-    RATE = 38.0e3
+    RATE = 33.0e3
     CORE_RATE = 700e3
     LATENCY = 2.6
     FAR_LATENCY = 3.6
@@ -371,16 +372,21 @@
             pack0[j, :, k * CH : (k + 1) * CH] = in_ref[BVC[k], :, j * CH : (j + 1) * CH]
         pack0[j, :, 3 * CH :] = out_ref[:, j * CH : (j + 1) * CH]
         cols, tile = slice(j * HALF, (j + 1) * HALF), slice(2048 + j // 2 * CH, 2048 + (j // 2 + 1) * CH)
-        for pack, k, ref in ((pack1, 0, gate_ref), (pack1, HP, up_ref), (pack2, 0, down_ref)):
-            pack[j, :, k : k + HALF] = ref[:, cols]
-            pack[j, :, k + HALF : k + HP] = half_tile(ref[:, tile].astype(F32), j % 2).astype(BF)
+        pack1[j, :, 0:HALF] = gate_ref[:, cols]
+        pack1[j, :, HALF : 2 * HALF] = up_ref[:, cols]
+        gate_half, up_half, down_half = [
+            half_tile(ref[:, tile].astype(F32), j % 2) for ref in (gate_ref, up_ref, down_ref)
+        ]
+        pack1[j, :, 2 * HALF :] = (gate_half + pltpu.roll(up_half, CH // 2, 1)).astype(BF)
+        pack2[j, :, 0:HALF] = down_ref[:, cols]
+        pack2[j, :, HALF:HP] = down_half.astype(BF)
     pl.semaphore_wait(barrier, len(others))
 
     s = Schedule(send_sems, recv_sems)
     packs, ws, gs = (pack0, pack1, pack1, pack2), (w0, w1, w1, w2), (g0, g1, g1, g2, g0)
     ras, rbs, oas = (ra0, ra1, ra2, ra3, ra4), (rb0, rb1, rb2, rb3, rb4), (oa0, oa1, oa1, oa2, oa0)
     outs = (g0_out, g1_out, g1_out, g2_out, g0_out)
-    lanes = (pl.ds(0, 512), pl.ds(0, HP), pl.ds(HP, HP), pl.ds(0, HP))
+    lanes = (pl.ds(0, 512), pl.ds(0, 512), pl.ds(512, HP), pl.ds(0, HP))
     grad_lanes = (pl.ds(2 * CH, 2 * CH),) + lanes[1:] + (pl.ds(0, 2 * CH),)
     my_cols = pl.ds(pl.multiple_of(core * HALF, HALF), HALF)
     peer_cols = pl.ds(pl.multiple_of((1 - core) * HALF, HALF), HALF)
@@ -645,14 +651,23 @@
 
     def ffn_block(j):
         rows = rows_of(j)
-        ab = nn(n2[rows, :], w1[...].reshape(D, 2 * HP))
-        a, b = ab[:, :HP], ab[:, HP:]
-        sg = jax.nn.sigmoid(a)
-        silu = a * sg
-        uu[rows, :] = (silu * b).astype(BF)
+        ab = nn(n2[rows, :], w1[...].reshape(D, GW))
         du = nn(dyf[rows, :], w2[...].reshape(D, HP))
-        dab[rows, 0:HP] = (du * b * sg * (1.0 + a * (1.0 - sg))).astype(BF)
-        dab[rows, HP : 2 * HP] = (du * silu).astype(BF)
+
+        def act(a, b, du):
+            sg = jax.nn.sigmoid(a)
+            silu = a * sg
+            return silu * b, du * b * sg * (1.0 + a * (1.0 - sg)), du * silu
+
+        u, da, db = act(ab[:, :HALF], ab[:, HALF : 2 * HALF], du[:, :HALF])
+        uu[rows, 0:HALF] = u.astype(BF)
+        dab[rows, 0:HALF] = da.astype(BF)
+        dab[rows, HALF : 2 * HALF] = db.astype(BF)
+        tile = ab[:, 2 * HALF :]
+        low = lax.broadcasted_iota(jnp.int32, (TOK, CH), 1) < CH // 2
+        u, da, db = [jnp.where(low, v, 0.0) for v in act(tile, pltpu.roll(tile, CH // 2, 1), du[:, HALF:])]
+        uu[rows, HALF:HP] = u.astype(BF)
+        dab[rows, 2 * HALF :] = (da + pltpu.roll(db, CH // 2, 1)).astype(BF)
         s.work(0.9)
 
     def y_part(j):
@@ -662,7 +677,7 @@
 
     def n2_part(j):
         rows = rows_of(j)
-        part = nt(dab[rows, :], w1[...].reshape(D, 2 * HP))
+        part = nt(dab[rows, :], w1[...].reshape(D, GW))
         zpart[1, rows, :] = part.astype(BF)
         small_out[pl.ds(1, 1), :] += jnp.sum(part * n2[rows, :].astype(F32), axis=0, keepdims=True)
         s.work(0.9)
@@ -811,7 +826,7 @@
     def make_half(h):
         def step(i):
             ln = lanes[1 + h]
-            g1[i, :, :, ln] = tn(n2[:, pl.ds(i * 256, 256)], dab[:, ln]).astype(BF).reshape(4, 64, HP)
+            g1[i, :, :, ln] = tn(n2[:, pl.ds(i * 256, 256)], dab[:, ln]).astype(BF).reshape(4, 64, ln.size)
             s.work(0.3)
 
         return step
@@ -899,12 +914,13 @@
         o_out[:, j * CH : (j + 1) * CH] = p0[j, :, 3 * CH :].astype(F32)
         cols = slice(j * HALF, (j + 1) * HALF)
         o_gate[:, cols] = p1[j, :, 0:HALF].astype(F32)
-        o_up[:, cols] = p1[j, :, HP : HP + HALF].astype(F32)
+        o_up[:, cols] = p1[j, :, HALF : 2 * HALF].astype(F32)
         o_down[:, cols] = p2[j, :, 0:HALF].astype(F32)
     for t in range(2):
         tile = slice(2048 + t * CH, 2048 + (t + 1) * CH)
-        o_gate[:, tile] = whole_tile(p1[2 * t, :, HALF:HP], p1[2 * t + 1, :, HALF:HP])
-        o_up[:, tile] = whole_tile(p1[2 * t, :, HP + HALF :], p1[2 * t + 1, :, HP + HALF :])
+        even, odd = [p1[2 * t + k, :, 2 * HALF :].astype(F32) for k in range(2)]
+        o_gate[:, tile] = whole_tile(even, odd)
+        o_up[:, tile] = jnp.where(low_lanes(), pltpu.roll(even, CH // 2, 1), odd)
         o_down[:, tile] = whole_tile(p2[2 * t, :, HALF:HP], p2[2 * t + 1, :, HALF:HP])
 
 
@@ -931,8 +947,8 @@
         loaded
         + plane
         + [pltpu.VMEM((4, 4, 64, w), BF) for w in WIDTHS]
-        + [pltpu.VMEM((2, 6, 4, 16, w), BF) for w in (2 * CH, HP, HP, HP, 2 * CH)]
-        + [pltpu.VMEM((2, 6, 16, w), BF) for w in (2 * CH, HP, HP, HP, 2 * CH)]
+        + [pltpu.VMEM((2, 6, 4, 16, w), BF) for w in (2 * CH, 512, HP, HP, 2 * CH)]
+        + [pltpu.VMEM((2, 6, 16, w), BF) for w in (2 * CH, 512, HP, HP, 2 * CH)]
         + [pltpu.VMEM((4, 16, w), BF) for w in WIDTHS]
         + [
             pltpu.VMEM((4, 8, CH), F32),
@@ -968,7 +984,7 @@
             pltpu.VMEM((2, 8, CH), F32),
             pltpu.VMEM((2, 8, CH), F32),
             pltpu.VMEM((GT, HP), BF),
-            pltpu.VMEM((GT, 2 * HP), BF),
+            pltpu.VMEM((GT, GW), BF),
             pltpu.VMEM((3, R, 8, HALF), F32),
             pltpu.VMEM((3, 8, HALF), F32),
             pltpu.VMEM((8, D), F32),

time: 104 us -> 103 us (level)
  no operation moved by 1% of the time
where the time goes in v5:
time: 103 us
  Pallas kernels  102 us (99%)
    pallas_call x1, Pallas kernels, block(): pl.pallas_call(kernel, out_shape=[jax.ShapeDtypeStruct((TOK, HALF), BF),...  99.8 us
    pallas_call x1, Pallas kernels, block(): pl.pallas_call(finish, out_shape=[jax.ShapeDtypeStruct((TOK, HALF), BF),...  2.12 us

profile of v5, /device:TPU:0, one launch (start us, length us, event | category | flops | bytes accessed | tf_op | source)
XLA Modules:
  0.0 102.6 jit_solution(3199129059817517348)
XLA Ops:
  0.6 99.8 %shard_map.195 = (bf16[128,512]{1,0:T(8,128)(2,1)}, f32[128,512]{1,0:T(8,128)}, f32[8,1024]{1,0:T(8,128)}, bf16[4,16,512]{2,1,0:T(8,128)(2,1)}, bf16[4,16,1152]{...) custom-call(bf16[128,512]{1,0:T(8,128)(2,1)} %tok_hbm.1, bf16[128,512]{1,0:T(8,128)(2,1)} %dy_hbm.1, s32[128]{0:T(128)} %seg_hbm.1, ...), custom_call_target="tpu_custom_call" | custom-call | tf_op jit(solution)/shard_map/pallas_call | solution.py:996
  100.4 2.1 %shard_map.196 = (bf16[128,512]{1,0:T(8,128)(2,1)}, f32[128,512]{1,0:T(8,128)}, f32[1024]{0:T(1024)}, f32[3,16,512]{2,1,0:T(8,128)}, f32[3,1024]{1,0:T(4,128)}, ...) custom-call(bf16[128,512]{1,0:T(8,128)(2,1)} %get-tuple-element.26.mix, ...), custom_call_target="tpu_custom_call" | custom-call | tf_op jit(solution)/shard_map/pallas_call | solution.py:1011
